TPU v7x, 32 devices: a whole 2x2x4 slice. The times are simulated.
32 devices in a mesh: panel: 16 (over z, x, core), freq: 2 (over y).
Axes of the slice: x: 2, y: 2, z: 4, core: 2. Of those that a mesh axis runs over, the one named last changes fastest.
Arguments:
- sources: bfloat16 [2, 4096, 1024], P(None, ('panel', 'freq')), may hold values from -6 to 6
- panel_pos: float32 [3, 4096], P(None, 'panel'), may hold values from -30 to 30
- normal_angles: float32 [2, 4096], P(None, 'panel'), may hold values from -3.140625 to 3.140625
- observer_angles: float32 [2, 2048], replicated, may hold values from -3.140625 to 3.140625
- absorption: float32 [64, 16], replicated, may hold values from 0.05 to 1
- ray_count: int32 [131072], P('panel'), may hold values from 1 to 8
- ray_layer: int32 [8, 131072], P(None, 'panel'), may hold values from 0 to 15
- ray_length: float32 [8, 131072], P(None, 'panel'), may hold values from 0.1 to 1
- ray_weight: float32 [131072], P('panel'), may hold values from 0.01 to 0.1
- ray_ground: int32 [131072], P('panel'), may hold values from 0 to 4095
Outputs:
- obs_spectrum: float32 [2048, 128], P('panel', 'freq')
- ground_power: float32 [64, 4096], P(None, 'panel')
All inputs are finite; a program needn't handle non-finite values.
Results may differ from a plain program's by a relative error of at most 0.0026.
Values may be sent and summed in bfloat16 or wider, within the bound.
A program may use at most 64 MiB of HBM per device.

v0:
```python
import math

import jax
import jax.numpy as jnp
from jax import lax
from jax.sharding import PartitionSpec as P

SAMPLES = 1024
FREQS = 64
BIN0 = 32
RAYS = 64
LAYERS = 16
GROUND = 4096


RADIUS = 150.0
GAIN = 3.0


def dft_table(samples, first_bin, nfreqs):
    sample_index = jnp.arange(samples, dtype=jnp.int32)
    bin_index = first_bin + jnp.arange(nfreqs, dtype=jnp.int32)
    phase_turns = sample_index[:, None] * bin_index[None, :] % samples
    phase_angle = 2.0 * math.pi / samples * phase_turns.astype(jnp.float32)
    window = 0.5 - 0.5 * jnp.cos(2.0 * math.pi / samples * sample_index.astype(jnp.float32))
    weighting = (window / math.sqrt(samples))[:, None]
    stacked = jnp.stack(
        [weighting * jnp.cos(phase_angle), -weighting * jnp.sin(phase_angle)], axis=2
    )
    return stacked.reshape(samples, 2 * nfreqs).astype(jnp.bfloat16)


def sphere_points(angles, radius, downward):
    polar_angle = angles[0]
    azimuth = angles[1]
    height = -jnp.cos(polar_angle) if downward else jnp.cos(polar_angle)
    return radius * jnp.stack(
        [jnp.sin(polar_angle) * jnp.cos(azimuth), jnp.sin(polar_angle) * jnp.sin(azimuth), height]
    )


def radiate(points, panel_pos, normals, wavenumbers, spectra, weighting):
    offset = points[:, :, None] - panel_pos[:, None, :]
    distance = jnp.sqrt(jnp.sum(offset * offset, axis=0))
    inverse = 1.0 / distance
    cosine = jnp.sum(offset * normals[:, None, :], axis=0) * inverse
    amplitude = RADIUS * weighting * inverse
    freq_count = wavenumbers.shape[0]
    per_freq = spectra.reshape(2, spectra.shape[1], freq_count, 2).transpose(2, 0, 1, 3)

    def one_freq(inputs):
        wavenumber, coeffs = inputs
        phase = wavenumber * distance
        cos_part = amplitude * jnp.cos(phase)
        sin_part = -amplitude * jnp.sin(phase)
        dip_real = cosine * (cos_part * inverse - wavenumber * sin_part)
        dip_imag = cosine * (sin_part * inverse + wavenumber * cos_part)
        mono_real = (-wavenumber * coeffs[0, :, 1])[None, :]
        mono_imag = (wavenumber * coeffs[0, :, 0])[None, :]
        load_real = coeffs[1, :, 0][None, :]
        load_imag = coeffs[1, :, 1][None, :]
        real_sum = jnp.sum(
            cos_part * mono_real
            - sin_part * mono_imag
            + dip_real * load_real
            - dip_imag * load_imag,
            axis=1,
        )
        imag_sum = jnp.sum(
            cos_part * mono_imag
            + sin_part * mono_real
            + dip_real * load_imag
            + dip_imag * load_real,
            axis=1,
        )
        return jnp.stack([real_sum, imag_sum], axis=1)

    result = lax.map(one_freq, (wavenumbers, per_freq))
    return result.transpose(1, 0, 2).reshape(points.shape[1], 2 * freq_count)


def layer_lengths(ray_count, ray_layer, ray_length):
    seg_rows = ray_layer.shape[0]
    segment = jnp.arange(seg_rows, dtype=jnp.int32)[:, None]
    used = jnp.where(segment < ray_count.reshape(1, -1), ray_length, 0.0)
    layer_ids = jnp.arange(LAYERS, dtype=jnp.int32)[None, :, None]
    matches = ray_layer.reshape(seg_rows, 1, -1) == layer_ids
    return jnp.sum(jnp.where(matches, used[:, None, :], 0.0), axis=0)


def ground_energy(power_rows, absorption, lengths, ray_weight, ray_ground, ground_count):
    optical_depth = jnp.dot(absorption, lengths, precision=lax.Precision.HIGHEST)
    freq_count = power_rows.shape[0]
    obs_count = power_rows.shape[1]
    shaped = optical_depth.reshape(freq_count, obs_count, RAYS)
    energy = power_rows[:, :, None] * ray_weight.reshape(1, obs_count, RAYS) * jnp.exp(-shaped)
    empty = jnp.zeros((freq_count, ground_count), jnp.float32)
    return empty.at[:, ray_ground].add(energy.reshape(freq_count, -1))


def power_of(spectrum_rows):
    real_part = spectrum_rows[:, 0::2]
    imaginary = spectrum_rows[:, 1::2]
    return (real_part * real_part + imaginary * imaginary).T


def shards(
    sources,
    panel_pos,
    normal_angles,
    observer_angles,
    absorption,
    ray_count,
    ray_layer,
    ray_length,
    ray_weight,
    ray_ground,
):
    freq_groups = lax.axis_size("freq")
    local_freqs = FREQS // freq_groups
    freq_start = lax.axis_index("freq") * local_freqs
    panel_rows = panel_pos.shape[1]
    transform_table = dft_table(SAMPLES, BIN0, FREQS)
    partial_value = jnp.dot(
        sources.reshape(-1, SAMPLES), transform_table, preferred_element_type=jnp.float32
    )
    partial_value = partial_value.reshape(2, sources.shape[1], 2 * FREQS)
    spectra = lax.all_to_all(partial_value, "freq", split_axis=2, concat_axis=1, tiled=True)
    freq_ids = freq_start + jnp.arange(local_freqs, dtype=jnp.int32)
    wavenumbers = (BIN0 + freq_ids).astype(jnp.float32) * (2.0 * math.pi / SAMPLES)
    points = sphere_points(observer_angles, RADIUS, True)
    normals = sphere_points(normal_angles, 1.0, False)
    weighting = GAIN / math.sqrt(panel_rows * lax.axis_size("panel"))
    obs_spectrum = lax.psum_scatter(
        radiate(points, panel_pos, normals, wavenumbers, spectra, weighting),
        "panel",
        scatter_dimension=0,
        tiled=True,
    )
    lengths = layer_lengths(ray_count, ray_layer, ray_length)
    own_absorption = lax.dynamic_slice_in_dim(absorption, freq_start, local_freqs, 0)
    ground_part = ground_energy(
        power_of(obs_spectrum), own_absorption, lengths, ray_weight, ray_ground, GROUND
    )
    ground_local = lax.psum_scatter(ground_part, "panel", scatter_dimension=1, tiled=True)
    ground_power = lax.all_gather(ground_local, "freq", axis=0, tiled=True)
    return (obs_spectrum, ground_power)


def solution(mesh):
    return jax.shard_map(
        shards,
        mesh=mesh,
        in_specs=(
            P(None, ("panel", "freq"), None),
            P(None, "panel"),
            P(None, "panel"),
            P(),
            P(),
            P("panel"),
            P(None, "panel"),
            P(None, "panel"),
            P("panel"),
            P("panel"),
        ),
        out_specs=(P("panel", "freq"), P(None, "panel")),
        check_vma=False,
    )
```

profile of v0, /device:TPU:0, one launch (start us, length us, event | category | flops | bytes accessed | tf_op | source)
XLA Modules:
  0.0 650.8 jit_solution(5006533582006477575)
XLA Ops:
  7.3 1.2 multiply_convert_fusion.1
  10.0 4.3 all-to-all-start
  14.9 1.5 fusion.2
  16.4 3.9 fusion.19
  20.6 439.8 %while.11 = (s32[]{:T(128)}, f32[32,2048,2]{1,2,0:T(2,128)S(1)}, f32[32]{0:T(128)S(1)}, f32[2048,256]{1,0:T(8,128)}, f32[2048,256]{1,0:T(8,128)}, /*index=5*/f32...) while((s32[]{:T(128)}, f32[32,2048,2]{1,2,0:T(2,128)S(1)}, ...), condition=%wide.region_5.6_spmd, body=%wide.region_2.5_spmd.sunk | while | flops 14156291 | bytes 10555533 | solution.py:78
  22.6 11.8 %subtract_reduce_fusion.2 = (f32[2048]{0:T(1024)S(1)}, f32[2048]{0:T(1024)S(1)}) fusion(f32[256]{0:T(256)S(1)} %bitcast.70, f32[256]{0:T(256)S(1)} %bitcast.71, f32[256]{0:T(256)S(1)} %bitcast.72, f32[256]{0:T(256)S(1)} %bitcast.69, f32[2048,256]{1,0:T(8,128)S(1)} %get-tuple-element.269, f32[]{:T(128)} %bitcast.54, ...), kind=kLoop, calls=%fused_computation.2.clone.1 | loop fusion | flops 14151680 | bytes 10506244 | tf_op jit(solution)/shard_map/while/body/eval_jaxpr/reduce_sum | solution.py:62
  36.3 11.8 %subtract_reduce_fusion.2 = (f32[2048]{0:T(1024)S(1)}, f32[2048]{0:T(1024)S(1)}) fusion(f32[256]{0:T(256)S(1)} %bitcast.70, f32[256]{0:T(256)S(1)} %bitcast.71, f32[256]{0:T(256)S(1)} %bitcast.72, f32[256]{0:T(256)S(1)} %bitcast.69, f32[2048,256]{1,0:T(8,128)S(1)} %get-tuple-element.269, f32[]{:T(128)} %bitcast.54, ...), kind=kLoop, calls=%fused_computation.2.clone.1 | loop fusion | flops 14151680 | bytes 10506244 | tf_op jit(solution)/shard_map/while/body/eval_jaxpr/reduce_sum | solution.py:62
  50.1 11.8 %subtract_reduce_fusion.2 = (f32[2048]{0:T(1024)S(1)}, f32[2048]{0:T(1024)S(1)}) fusion(f32[256]{0:T(256)S(1)} %bitcast.70, f32[256]{0:T(256)S(1)} %bitcast.71, f32[256]{0:T(256)S(1)} %bitcast.72, f32[256]{0:T(256)S(1)} %bitcast.69, f32[2048,256]{1,0:T(8,128)S(1)} %get-tuple-element.269, f32[]{:T(128)} %bitcast.54, ...), kind=kLoop, calls=%fused_computation.2.clone.1 | loop fusion | flops 14151680 | bytes 10506244 | tf_op jit(solution)/shard_map/while/body/eval_jaxpr/reduce_sum | solution.py:62
  63.8 11.8 %subtract_reduce_fusion.2 = (f32[2048]{0:T(1024)S(1)}, f32[2048]{0:T(1024)S(1)}) fusion(f32[256]{0:T(256)S(1)} %bitcast.70, f32[256]{0:T(256)S(1)} %bitcast.71, f32[256]{0:T(256)S(1)} %bitcast.72, f32[256]{0:T(256)S(1)} %bitcast.69, f32[2048,256]{1,0:T(8,128)S(1)} %get-tuple-element.269, f32[]{:T(128)} %bitcast.54, ...), kind=kLoop, calls=%fused_computation.2.clone.1 | loop fusion | flops 14151680 | bytes 10506244 | tf_op jit(solution)/shard_map/while/body/eval_jaxpr/reduce_sum | solution.py:62
  77.5 11.8 %subtract_reduce_fusion.2 = (f32[2048]{0:T(1024)S(1)}, f32[2048]{0:T(1024)S(1)}) fusion(f32[256]{0:T(256)S(1)} %bitcast.70, f32[256]{0:T(256)S(1)} %bitcast.71, f32[256]{0:T(256)S(1)} %bitcast.72, f32[256]{0:T(256)S(1)} %bitcast.69, f32[2048,256]{1,0:T(8,128)S(1)} %get-tuple-element.269, f32[]{:T(128)} %bitcast.54, ...), kind=kLoop, calls=%fused_computation.2.clone.1 | loop fusion | flops 14151680 | bytes 10506244 | tf_op jit(solution)/shard_map/while/body/eval_jaxpr/reduce_sum | solution.py:62
  91.3 11.8 %subtract_reduce_fusion.2 = (f32[2048]{0:T(1024)S(1)}, f32[2048]{0:T(1024)S(1)}) fusion(f32[256]{0:T(256)S(1)} %bitcast.70, f32[256]{0:T(256)S(1)} %bitcast.71, f32[256]{0:T(256)S(1)} %bitcast.72, f32[256]{0:T(256)S(1)} %bitcast.69, f32[2048,256]{1,0:T(8,128)S(1)} %get-tuple-element.269, f32[]{:T(128)} %bitcast.54, ...), kind=kLoop, calls=%fused_computation.2.clone.1 | loop fusion | flops 14151680 | bytes 10506244 | tf_op jit(solution)/shard_map/while/body/eval_jaxpr/reduce_sum | solution.py:62
  105.0 11.8 %subtract_reduce_fusion.2 = (f32[2048]{0:T(1024)S(1)}, f32[2048]{0:T(1024)S(1)}) fusion(f32[256]{0:T(256)S(1)} %bitcast.70, f32[256]{0:T(256)S(1)} %bitcast.71, f32[256]{0:T(256)S(1)} %bitcast.72, f32[256]{0:T(256)S(1)} %bitcast.69, f32[2048,256]{1,0:T(8,128)S(1)} %get-tuple-element.269, f32[]{:T(128)} %bitcast.54, ...), kind=kLoop, calls=%fused_computation.2.clone.1 | loop fusion | flops 14151680 | bytes 10506244 | tf_op jit(solution)/shard_map/while/body/eval_jaxpr/reduce_sum | solution.py:62
  118.8 11.8 %subtract_reduce_fusion.2 = (f32[2048]{0:T(1024)S(1)}, f32[2048]{0:T(1024)S(1)}) fusion(f32[256]{0:T(256)S(1)} %bitcast.70, f32[256]{0:T(256)S(1)} %bitcast.71, f32[256]{0:T(256)S(1)} %bitcast.72, f32[256]{0:T(256)S(1)} %bitcast.69, f32[2048,256]{1,0:T(8,128)S(1)} %get-tuple-element.269, f32[]{:T(128)} %bitcast.54, ...), kind=kLoop, calls=%fused_computation.2.clone.1 | loop fusion | flops 14151680 | bytes 10506244 | tf_op jit(solution)/shard_map/while/body/eval_jaxpr/reduce_sum | solution.py:62
  132.5 11.8 %subtract_reduce_fusion.2 = (f32[2048]{0:T(1024)S(1)}, f32[2048]{0:T(1024)S(1)}) fusion(f32[256]{0:T(256)S(1)} %bitcast.70, f32[256]{0:T(256)S(1)} %bitcast.71, f32[256]{0:T(256)S(1)} %bitcast.72, f32[256]{0:T(256)S(1)} %bitcast.69, f32[2048,256]{1,0:T(8,128)S(1)} %get-tuple-element.269, f32[]{:T(128)} %bitcast.54, ...), kind=kLoop, calls=%fused_computation.2.clone.1 | loop fusion | flops 14151680 | bytes 10506244 | tf_op jit(solution)/shard_map/while/body/eval_jaxpr/reduce_sum | solution.py:62
  146.3 11.8 %subtract_reduce_fusion.2 = (f32[2048]{0:T(1024)S(1)}, f32[2048]{0:T(1024)S(1)}) fusion(f32[256]{0:T(256)S(1)} %bitcast.70, f32[256]{0:T(256)S(1)} %bitcast.71, f32[256]{0:T(256)S(1)} %bitcast.72, f32[256]{0:T(256)S(1)} %bitcast.69, f32[2048,256]{1,0:T(8,128)S(1)} %get-tuple-element.269, f32[]{:T(128)} %bitcast.54, ...), kind=kLoop, calls=%fused_computation.2.clone.1 | loop fusion | flops 14151680 | bytes 10506244 | tf_op jit(solution)/shard_map/while/body/eval_jaxpr/reduce_sum | solution.py:62
  160.0 11.8 %subtract_reduce_fusion.2 = (f32[2048]{0:T(1024)S(1)}, f32[2048]{0:T(1024)S(1)}) fusion(f32[256]{0:T(256)S(1)} %bitcast.70, f32[256]{0:T(256)S(1)} %bitcast.71, f32[256]{0:T(256)S(1)} %bitcast.72, f32[256]{0:T(256)S(1)} %bitcast.69, f32[2048,256]{1,0:T(8,128)S(1)} %get-tuple-element.269, f32[]{:T(128)} %bitcast.54, ...), kind=kLoop, calls=%fused_computation.2.clone.1 | loop fusion | flops 14151680 | bytes 10506244 | tf_op jit(solution)/shard_map/while/body/eval_jaxpr/reduce_sum | solution.py:62
  173.7 11.8 %subtract_reduce_fusion.2 = (f32[2048]{0:T(1024)S(1)}, f32[2048]{0:T(1024)S(1)}) fusion(f32[256]{0:T(256)S(1)} %bitcast.70, f32[256]{0:T(256)S(1)} %bitcast.71, f32[256]{0:T(256)S(1)} %bitcast.72, f32[256]{0:T(256)S(1)} %bitcast.69, f32[2048,256]{1,0:T(8,128)S(1)} %get-tuple-element.269, f32[]{:T(128)} %bitcast.54, ...), kind=kLoop, calls=%fused_computation.2.clone.1 | loop fusion | flops 14151680 | bytes 10506244 | tf_op jit(solution)/shard_map/while/body/eval_jaxpr/reduce_sum | solution.py:62
  187.5 11.8 %subtract_reduce_fusion.2 = (f32[2048]{0:T(1024)S(1)}, f32[2048]{0:T(1024)S(1)}) fusion(f32[256]{0:T(256)S(1)} %bitcast.70, f32[256]{0:T(256)S(1)} %bitcast.71, f32[256]{0:T(256)S(1)} %bitcast.72, f32[256]{0:T(256)S(1)} %bitcast.69, f32[2048,256]{1,0:T(8,128)S(1)} %get-tuple-element.269, f32[]{:T(128)} %bitcast.54, ...), kind=kLoop, calls=%fused_computation.2.clone.1 | loop fusion | flops 14151680 | bytes 10506244 | tf_op jit(solution)/shard_map/while/body/eval_jaxpr/reduce_sum | solution.py:62
  201.2 11.8 %subtract_reduce_fusion.2 = (f32[2048]{0:T(1024)S(1)}, f32[2048]{0:T(1024)S(1)}) fusion(f32[256]{0:T(256)S(1)} %bitcast.70, f32[256]{0:T(256)S(1)} %bitcast.71, f32[256]{0:T(256)S(1)} %bitcast.72, f32[256]{0:T(256)S(1)} %bitcast.69, f32[2048,256]{1,0:T(8,128)S(1)} %get-tuple-element.269, f32[]{:T(128)} %bitcast.54, ...), kind=kLoop, calls=%fused_computation.2.clone.1 | loop fusion | flops 14151680 | bytes 10506244 | tf_op jit(solution)/shard_map/while/body/eval_jaxpr/reduce_sum | solution.py:62
  215.0 11.8 %subtract_reduce_fusion.2 = (f32[2048]{0:T(1024)S(1)}, f32[2048]{0:T(1024)S(1)}) fusion(f32[256]{0:T(256)S(1)} %bitcast.70, f32[256]{0:T(256)S(1)} %bitcast.71, f32[256]{0:T(256)S(1)} %bitcast.72, f32[256]{0:T(256)S(1)} %bitcast.69, f32[2048,256]{1,0:T(8,128)S(1)} %get-tuple-element.269, f32[]{:T(128)} %bitcast.54, ...), kind=kLoop, calls=%fused_computation.2.clone.1 | loop fusion | flops 14151680 | bytes 10506244 | tf_op jit(solution)/shard_map/while/body/eval_jaxpr/reduce_sum | solution.py:62
  228.7 11.8 %subtract_reduce_fusion.2 = (f32[2048]{0:T(1024)S(1)}, f32[2048]{0:T(1024)S(1)}) fusion(f32[256]{0:T(256)S(1)} %bitcast.70, f32[256]{0:T(256)S(1)} %bitcast.71, f32[256]{0:T(256)S(1)} %bitcast.72, f32[256]{0:T(256)S(1)} %bitcast.69, f32[2048,256]{1,0:T(8,128)S(1)} %get-tuple-element.269, f32[]{:T(128)} %bitcast.54, ...), kind=kLoop, calls=%fused_computation.2.clone.1 | loop fusion | flops 14151680 | bytes 10506244 | tf_op jit(solution)/shard_map/while/body/eval_jaxpr/reduce_sum | solution.py:62
  242.5 11.8 %subtract_reduce_fusion.2 = (f32[2048]{0:T(1024)S(1)}, f32[2048]{0:T(1024)S(1)}) fusion(f32[256]{0:T(256)S(1)} %bitcast.70, f32[256]{0:T(256)S(1)} %bitcast.71, f32[256]{0:T(256)S(1)} %bitcast.72, f32[256]{0:T(256)S(1)} %bitcast.69, f32[2048,256]{1,0:T(8,128)S(1)} %get-tuple-element.269, f32[]{:T(128)} %bitcast.54, ...), kind=kLoop, calls=%fused_computation.2.clone.1 | loop fusion | flops 14151680 | bytes 10506244 | tf_op jit(solution)/shard_map/while/body/eval_jaxpr/reduce_sum | solution.py:62
  256.2 11.8 %subtract_reduce_fusion.2 = (f32[2048]{0:T(1024)S(1)}, f32[2048]{0:T(1024)S(1)}) fusion(f32[256]{0:T(256)S(1)} %bitcast.70, f32[256]{0:T(256)S(1)} %bitcast.71, f32[256]{0:T(256)S(1)} %bitcast.72, f32[256]{0:T(256)S(1)} %bitcast.69, f32[2048,256]{1,0:T(8,128)S(1)} %get-tuple-element.269, f32[]{:T(128)} %bitcast.54, ...), kind=kLoop, calls=%fused_computation.2.clone.1 | loop fusion | flops 14151680 | bytes 10506244 | tf_op jit(solution)/shard_map/while/body/eval_jaxpr/reduce_sum | solution.py:62
  270.0 11.8 %subtract_reduce_fusion.2 = (f32[2048]{0:T(1024)S(1)}, f32[2048]{0:T(1024)S(1)}) fusion(f32[256]{0:T(256)S(1)} %bitcast.70, f32[256]{0:T(256)S(1)} %bitcast.71, f32[256]{0:T(256)S(1)} %bitcast.72, f32[256]{0:T(256)S(1)} %bitcast.69, f32[2048,256]{1,0:T(8,128)S(1)} %get-tuple-element.269, f32[]{:T(128)} %bitcast.54, ...), kind=kLoop, calls=%fused_computation.2.clone.1 | loop fusion | flops 14151680 | bytes 10506244 | tf_op jit(solution)/shard_map/while/body/eval_jaxpr/reduce_sum | solution.py:62
  283.7 11.8 %subtract_reduce_fusion.2 = (f32[2048]{0:T(1024)S(1)}, f32[2048]{0:T(1024)S(1)}) fusion(f32[256]{0:T(256)S(1)} %bitcast.70, f32[256]{0:T(256)S(1)} %bitcast.71, f32[256]{0:T(256)S(1)} %bitcast.72, f32[256]{0:T(256)S(1)} %bitcast.69, f32[2048,256]{1,0:T(8,128)S(1)} %get-tuple-element.269, f32[]{:T(128)} %bitcast.54, ...), kind=kLoop, calls=%fused_computation.2.clone.1 | loop fusion | flops 14151680 | bytes 10506244 | tf_op jit(solution)/shard_map/while/body/eval_jaxpr/reduce_sum | solution.py:62
  297.4 11.8 %subtract_reduce_fusion.2 = (f32[2048]{0:T(1024)S(1)}, f32[2048]{0:T(1024)S(1)}) fusion(f32[256]{0:T(256)S(1)} %bitcast.70, f32[256]{0:T(256)S(1)} %bitcast.71, f32[256]{0:T(256)S(1)} %bitcast.72, f32[256]{0:T(256)S(1)} %bitcast.69, f32[2048,256]{1,0:T(8,128)S(1)} %get-tuple-element.269, f32[]{:T(128)} %bitcast.54, ...), kind=kLoop, calls=%fused_computation.2.clone.1 | loop fusion | flops 14151680 | bytes 10506244 | tf_op jit(solution)/shard_map/while/body/eval_jaxpr/reduce_sum | solution.py:62
  311.2 11.8 %subtract_reduce_fusion.2 = (f32[2048]{0:T(1024)S(1)}, f32[2048]{0:T(1024)S(1)}) fusion(f32[256]{0:T(256)S(1)} %bitcast.70, f32[256]{0:T(256)S(1)} %bitcast.71, f32[256]{0:T(256)S(1)} %bitcast.72, f32[256]{0:T(256)S(1)} %bitcast.69, f32[2048,256]{1,0:T(8,128)S(1)} %get-tuple-element.269, f32[]{:T(128)} %bitcast.54, ...), kind=kLoop, calls=%fused_computation.2.clone.1 | loop fusion | flops 14151680 | bytes 10506244 | tf_op jit(solution)/shard_map/while/body/eval_jaxpr/reduce_sum | solution.py:62
  324.9 11.8 %subtract_reduce_fusion.2 = (f32[2048]{0:T(1024)S(1)}, f32[2048]{0:T(1024)S(1)}) fusion(f32[256]{0:T(256)S(1)} %bitcast.70, f32[256]{0:T(256)S(1)} %bitcast.71, f32[256]{0:T(256)S(1)} %bitcast.72, f32[256]{0:T(256)S(1)} %bitcast.69, f32[2048,256]{1,0:T(8,128)S(1)} %get-tuple-element.269, f32[]{:T(128)} %bitcast.54, ...), kind=kLoop, calls=%fused_computation.2.clone.1 | loop fusion | flops 14151680 | bytes 10506244 | tf_op jit(solution)/shard_map/while/body/eval_jaxpr/reduce_sum | solution.py:62
  338.7 11.8 %subtract_reduce_fusion.2 = (f32[2048]{0:T(1024)S(1)}, f32[2048]{0:T(1024)S(1)}) fusion(f32[256]{0:T(256)S(1)} %bitcast.70, f32[256]{0:T(256)S(1)} %bitcast.71, f32[256]{0:T(256)S(1)} %bitcast.72, f32[256]{0:T(256)S(1)} %bitcast.69, f32[2048,256]{1,0:T(8,128)S(1)} %get-tuple-element.269, f32[]{:T(128)} %bitcast.54, ...), kind=kLoop, calls=%fused_computation.2.clone.1 | loop fusion | flops 14151680 | bytes 10506244 | tf_op jit(solution)/shard_map/while/body/eval_jaxpr/reduce_sum | solution.py:62
  352.4 11.8 %subtract_reduce_fusion.2 = (f32[2048]{0:T(1024)S(1)}, f32[2048]{0:T(1024)S(1)}) fusion(f32[256]{0:T(256)S(1)} %bitcast.70, f32[256]{0:T(256)S(1)} %bitcast.71, f32[256]{0:T(256)S(1)} %bitcast.72, f32[256]{0:T(256)S(1)} %bitcast.69, f32[2048,256]{1,0:T(8,128)S(1)} %get-tuple-element.269, f32[]{:T(128)} %bitcast.54, ...), kind=kLoop, calls=%fused_computation.2.clone.1 | loop fusion | flops 14151680 | bytes 10506244 | tf_op jit(solution)/shard_map/while/body/eval_jaxpr/reduce_sum | solution.py:62
  366.2 11.8 %subtract_reduce_fusion.2 = (f32[2048]{0:T(1024)S(1)}, f32[2048]{0:T(1024)S(1)}) fusion(f32[256]{0:T(256)S(1)} %bitcast.70, f32[256]{0:T(256)S(1)} %bitcast.71, f32[256]{0:T(256)S(1)} %bitcast.72, f32[256]{0:T(256)S(1)} %bitcast.69, f32[2048,256]{1,0:T(8,128)S(1)} %get-tuple-element.269, f32[]{:T(128)} %bitcast.54, ...), kind=kLoop, calls=%fused_computation.2.clone.1 | loop fusion | flops 14151680 | bytes 10506244 | tf_op jit(solution)/shard_map/while/body/eval_jaxpr/reduce_sum | solution.py:62
  379.9 11.8 %subtract_reduce_fusion.2 = (f32[2048]{0:T(1024)S(1)}, f32[2048]{0:T(1024)S(1)}) fusion(f32[256]{0:T(256)S(1)} %bitcast.70, f32[256]{0:T(256)S(1)} %bitcast.71, f32[256]{0:T(256)S(1)} %bitcast.72, f32[256]{0:T(256)S(1)} %bitcast.69, f32[2048,256]{1,0:T(8,128)S(1)} %get-tuple-element.269, f32[]{:T(128)} %bitcast.54, ...), kind=kLoop, calls=%fused_computation.2.clone.1 | loop fusion | flops 14151680 | bytes 10506244 | tf_op jit(solution)/shard_map/while/body/eval_jaxpr/reduce_sum | solution.py:62
  393.6 11.8 %subtract_reduce_fusion.2 = (f32[2048]{0:T(1024)S(1)}, f32[2048]{0:T(1024)S(1)}) fusion(f32[256]{0:T(256)S(1)} %bitcast.70, f32[256]{0:T(256)S(1)} %bitcast.71, f32[256]{0:T(256)S(1)} %bitcast.72, f32[256]{0:T(256)S(1)} %bitcast.69, f32[2048,256]{1,0:T(8,128)S(1)} %get-tuple-element.269, f32[]{:T(128)} %bitcast.54, ...), kind=kLoop, calls=%fused_computation.2.clone.1 | loop fusion | flops 14151680 | bytes 10506244 | tf_op jit(solution)/shard_map/while/body/eval_jaxpr/reduce_sum | solution.py:62
  407.4 11.8 %subtract_reduce_fusion.2 = (f32[2048]{0:T(1024)S(1)}, f32[2048]{0:T(1024)S(1)}) fusion(f32[256]{0:T(256)S(1)} %bitcast.70, f32[256]{0:T(256)S(1)} %bitcast.71, f32[256]{0:T(256)S(1)} %bitcast.72, f32[256]{0:T(256)S(1)} %bitcast.69, f32[2048,256]{1,0:T(8,128)S(1)} %get-tuple-element.269, f32[]{:T(128)} %bitcast.54, ...), kind=kLoop, calls=%fused_computation.2.clone.1 | loop fusion | flops 14151680 | bytes 10506244 | tf_op jit(solution)/shard_map/while/body/eval_jaxpr/reduce_sum | solution.py:62
  421.1 11.8 %subtract_reduce_fusion.2 = (f32[2048]{0:T(1024)S(1)}, f32[2048]{0:T(1024)S(1)}) fusion(f32[256]{0:T(256)S(1)} %bitcast.70, f32[256]{0:T(256)S(1)} %bitcast.71, f32[256]{0:T(256)S(1)} %bitcast.72, f32[256]{0:T(256)S(1)} %bitcast.69, f32[2048,256]{1,0:T(8,128)S(1)} %get-tuple-element.269, f32[]{:T(128)} %bitcast.54, ...), kind=kLoop, calls=%fused_computation.2.clone.1 | loop fusion | flops 14151680 | bytes 10506244 | tf_op jit(solution)/shard_map/while/body/eval_jaxpr/reduce_sum | solution.py:62
  434.9 11.8 %subtract_reduce_fusion.2 = (f32[2048]{0:T(1024)S(1)}, f32[2048]{0:T(1024)S(1)}) fusion(f32[256]{0:T(256)S(1)} %bitcast.70, f32[256]{0:T(256)S(1)} %bitcast.71, f32[256]{0:T(256)S(1)} %bitcast.72, f32[256]{0:T(256)S(1)} %bitcast.69, f32[2048,256]{1,0:T(8,128)S(1)} %get-tuple-element.269, f32[]{:T(128)} %bitcast.54, ...), kind=kLoop, calls=%fused_computation.2.clone.1 | loop fusion | flops 14151680 | bytes 10506244 | tf_op jit(solution)/shard_map/while/body/eval_jaxpr/reduce_sum | solution.py:62
  448.6 11.8 %subtract_reduce_fusion.2 = (f32[2048]{0:T(1024)S(1)}, f32[2048]{0:T(1024)S(1)}) fusion(f32[256]{0:T(256)S(1)} %bitcast.70, f32[256]{0:T(256)S(1)} %bitcast.71, f32[256]{0:T(256)S(1)} %bitcast.72, f32[256]{0:T(256)S(1)} %bitcast.69, f32[2048,256]{1,0:T(8,128)S(1)} %get-tuple-element.269, f32[]{:T(128)} %bitcast.54, ...), kind=kLoop, calls=%fused_computation.2.clone.1 | loop fusion | flops 14151680 | bytes 10506244 | tf_op jit(solution)/shard_map/while/body/eval_jaxpr/reduce_sum | solution.py:62
  460.4 1.2 reshape.245
  461.9 0.8 fusion.13
  464.2 56.1 %reduce-scatter.3.cloned.1.call-done = f32[128,64]{0,1:T(8,128)} async-done(((f32[2048,64]{0,1:T(8,128)}), f32[128,64]{0,1:T(8,128)}) %reduce-scatter.3.cloned.1.call-update) | async-done | bytes 32784 | tf_op jit(solution)/shard_map/reduce_scatter | solution.py:134
  521.8 2.2 fusion.4
  524.0 1.8 copy.49
  525.8 1.6 reshape.248
  527.5 3.6 copy.50
  531.0 45.7 %scatter_custom_fusion = f32[32,4096]{0,1:T(8,128)} fusion(s32[8192]{0:T(1024)S(1)} %compare_select_fusion, f32[8192,32]{1,0:T(8,128)} %copy.50, f32[]{:T(128)} %constant.23.clone.1), kind=kCustom, calls=%fused_computation.22 | custom fusion | flops 262144 | bytes 524800 | tf_op jit(solution)/shard_map/scatter-add | solution.py:98
  576.8 61.0 %reduce-scatter.5.cloned.1.call-done = f32[32,256]{0,1:T(8,128)} async-done(((f32[32,4096]{0,1:T(8,128)}), f32[32,256]{0,1:T(8,128)}) %reduce-scatter.5.cloned.1.call-update) | async-done | bytes 32784 | tf_op jit(solution)/shard_map/reduce_scatter | solution.py:145
  637.8 1.0 copy.51
  638.7 4.6 all_gather.3
  (177 shorter events, 47.3 us)
Async XLA Ops:
  7.2 1.8 copy-start
  7.2 7.1 %copy-start.5 = (f32[2,2048]{1,0:T(2,128)S(1)}, f32[2,2048]{1,0:T(2,128)}, u32[]{:S(2)}) copy-start(f32[2,2048]{1,0:T(2,128)} %param.15) | copy-start | bytes 49156
  7.2 7.6 %copy-start.8 = (f32[2,256]{1,0:T(2,128)S(1)}, f32[2,256]{1,0:T(2,128)}, u32[]{:S(2)}) copy-start(f32[2,256]{1,0:T(2,128)} %param.14) | copy-start | bytes 6148
  7.2 7.7 %copy-start.7 = (f32[3,256]{1,0:T(4,128)S(1)}, f32[3,256]{1,0:T(4,128)}, u32[]{:S(2)}) copy-start(f32[3,256]{1,0:T(4,128)} %param.13) | copy-start | bytes 9220
  10.0 10.3 %all-to-all-start = ((f32[2,128,128]{1,0,2:T(2,128)}), f32[2,128,128]{1,0,2:T(2,128)S(1)}, u32[]{:S(2)}, u32[]{:S(2)}) async-start(f32[2,128,128]{1,0,2:T(2,128)} %reshape.243), calls=%async_computation | async-start | bytes 262144 | tf_op jit(solution)/shard_map/all_to_all | solution.py:128
  14.3 506.0 %reduce-scatter.3.cloned.1.call-start = ((), (), s32[]{:S(2)}) async-start(), calls=%async_computation.3 | async-start | bytes 557056 | tf_op jit(solution)/shard_map/reduce_scatter | solution.py:134
  20.6 441.2 %copy-start.1 = (f32[8,8192]{1,0:T(8,128)S(1)}, f32[8,8192]{1,0:T(8,128)}, u32[]{:S(2)}) copy-start(f32[8,8192]{1,0:T(8,128)} %param.19) | copy-start | bytes 786436
  460.4 2.2 copy-start.2
  461.6 176.1 %reduce-scatter.5.cloned.1.call-start = ((), (), s32[]{:S(2)}) async-start(), calls=%async_computation.4 | async-start | bytes 2228224 | tf_op jit(solution)/shard_map/reduce_scatter | solution.py:145
  462.7 1.4 copy-start.3
  462.7 1.5 copy-start.4
  462.7 59.1 %copy-start.6 = (f32[64,16]{0,1:T(8,128)S(1)}, f32[64,16]{0,1:T(8,128)}, u32[]{:S(2)}) copy-start(f32[64,16]{0,1:T(8,128)} %param.16) | copy-start | bytes 12292
Sparse Core Ops, SparseCore 0:
  461.7 58.4 reduce-scatter.2
  576.9 60.8 reduce-scatter.4
where the time goes:
time: 655 us; the launch traced here: 651 us
  other arithmetic  453 us (69%)
  waiting for transfers between devices  117 us (18%)
  local copies, waits for them, and re-layouts  32.8 us (5%)
  loops' own time  22 us (3%)
  between operations  14.3 us (2%)
    reduce_sum x32, other arithmetic, one_freq(): jnp.sum(cos_part * mono_real - sin_part * mono_imag + dip_real * load_rea...  377 us
    reduce_scatter x1, waiting for transfers between devices, shards(): lax.psum_scatter(ground_part, 'panel', scatter_dimension=1, tiled=True)  61 us
    reduce_scatter x1, waiting for transfers between devices, shards(): lax.psum_scatter(radiate(points, panel_pos, normals, wavenumbers, spectra...  56.1 us
    scatter-add x1, other arithmetic, ground_energy(): return empty.at[:, ray_ground].add(energy.reshape(freq_count, -1))  45.7 us
    another operation x1, loops' own time, radiate(): result = lax.map(one_freq, (wavenumbers, per_freq))  22 us
    mul x32, other arithmetic, one_freq(): mono_real = (-wavenumber * coeffs[0, :, 1])[None, :]  20.9 us
    dynamic_slice x32, local copies, waits for them, and re-layouts, radiate(): result = lax.map(one_freq, (wavenumbers, per_freq))  18.8 us
  transfers between devices with their start and end apart: 3, of which 2 were waited for; matrix products, arithmetic and copies ran while one was open for 1% of the time, Pallas kernels for 0%

commit v1 on v0

v1 whole, which is shorter than its diff:
```python
import functools
import math

import jax
import jax.numpy as jnp
import numpy as np
from jax import lax
from jax.experimental import pallas as pl
from jax.experimental.pallas import tpu as pltpu
from jax.sharding import PartitionSpec as P

SAMPLES = 1024
BIN0 = 32
RADIUS = 150.0
GAIN = 3.0
GROUND = 4096
TILE = 16
MESH = pl.DeviceIdType.MESH
VMEM = pltpu.MemorySpace.VMEM


def dft_rows(samples, first_bin, groups, per_group):
    index = np.arange(samples)
    bins = first_bin + np.arange(groups * per_group)
    angle = 2.0 * np.pi / samples * (bins[:, None] * index[None, :] % samples)
    window = (0.5 - 0.5 * np.cos(2.0 * np.pi / samples * index)) / math.sqrt(samples)
    rows = np.stack([window * np.cos(angle), -window * np.sin(angle)])
    rows = rows.reshape(2, groups, per_group, samples).transpose(1, 0, 2, 3)
    return rows.reshape(-1, samples).astype(np.float32)


def sphere_points(angles, downward):
    polar, azimuth = angles[0], angles[1]
    height = -jnp.cos(polar) if downward else jnp.cos(polar)
    return jnp.stack(
        [jnp.sin(polar) * jnp.cos(azimuth), jnp.sin(polar) * jnp.sin(azimuth), height]
    )


def sincos_turns(turns):
    part = turns - jnp.round(turns)
    square = part * part
    sine = jnp.float32(-(math.pi**11) / math.factorial(11))
    for power in (9, 7, 5, 3, 1):
        sign = 1.0 if power % 4 == 1 else -1.0
        sine = sine * square + sign * math.pi**power / math.factorial(power)
    sine = sine * part
    cosine = jnp.float32(math.pi**12 / math.factorial(12))
    for power in (10, 8, 6, 4, 2, 0):
        sign = 1.0 if power % 4 == 0 else -1.0
        cosine = cosine * square + sign * math.pi**power / math.factorial(power)
    return 1.0 - 2.0 * sine * sine, 2.0 * sine * cosine


def radiate_kernel(freqs, panels, width, blocks, first_ref, pos_ref, points_ref, coef_ref,
                   out_ref, planes_a, planes_b, stage):
    tiles = panels // TILE
    half = width // out_ref.shape[2]
    lanes = out_ref.shape[2]

    def generate(planes, block, tile):
        rows = pl.ds(pl.multiple_of(tile * TILE, TILE), TILE)
        cols = pl.ds(pl.multiple_of(block * width, width), width)
        total = None
        for axis in range(3):
            diff = points_ref[axis : axis + 1, cols] - pos_ref[rows, axis : axis + 1]
            total = diff * diff if total is None else total + diff * diff
        inverse = lax.rsqrt(total)
        inverse = inverse * (1.5 - 0.5 * total * inverse * inverse)
        turn = total * inverse * jnp.float32(RADIUS / SAMPLES)
        cos_step, sin_step = sincos_turns(turn)
        cos_now, sin_now = sincos_turns(turn * first_ref[0:1, 0:1])
        square = inverse * inverse
        cube = square * inverse
        cos_next = cos_now * cos_step - sin_now * sin_step
        sin_next = sin_now * cos_step + cos_now * sin_step
        twice = 2.0 * cos_step
        before = [cos_now * cube, sin_now * cube, cos_now * square, sin_now * square]
        current = [cos_next * cube, sin_next * cube, cos_next * square, sin_next * square]
        for f in range(freqs):
            for part in range(4):
                at = pl.ds(pl.multiple_of(part * panels + tile * TILE, TILE), TILE)
                planes[f, at, :] = before[part].astype(jnp.bfloat16)
            if f + 1 < freqs:
                before, current = current, [
                    twice * now - old for now, old in zip(current, before)
                ]

    def contract(planes, block, f):
        cols = pl.ds(pl.multiple_of(block * width, width), width)
        product = jnp.dot(coef_ref[f], planes[f], preferred_element_type=jnp.float32)
        product = (product[0:8] + product[8:16]) * points_ref[8:16, cols]
        product = product + pltpu.roll(product, 1, axis=0)
        product = product + pltpu.roll(product, 2, axis=0)
        for side in range(half):
            stage[side, pl.ds(pl.multiple_of(f * 8, 8), 8), :] = product[
                :, side * lanes : (side + 1) * lanes
            ]

    def finish(block):
        for part in range(2):
            for side in range(half):
                out_ref[block * half + side, part * freqs : (part + 1) * freqs, :] = stage[
                    side, pl.ds(4 * part + 3, freqs, 8), :
                ]

    def phase(generated, generated_block, used, used_block):
        if generated is not None and used is not None and freqs % tiles == 0:
            each = freqs // tiles

            def both(tile, carry):
                for n in range(each):
                    contract(used, used_block, tile * each + n)
                generate(generated, generated_block, tile)
                return carry

            lax.fori_loop(0, tiles, both, 0)
            finish(used_block)
            return
        if generated is not None:

            def only_generate(tile, carry):
                generate(generated, generated_block, tile)
                return carry

            lax.fori_loop(0, tiles, only_generate, 0)
        if used is not None:

            def only_contract(f, carry):
                contract(used, used_block, f)
                return carry

            lax.fori_loop(0, freqs, only_contract, 0)
            finish(used_block)

    phase(planes_a, 0, None, None)

    def pair(step, carry):
        phase(planes_b, 2 * step + 1, planes_a, 2 * step)
        phase(planes_a, 2 * step + 2, planes_b, 2 * step + 1)
        return carry

    lax.fori_loop(0, blocks // 2 - 1, pair, 0)
    phase(planes_b, blocks - 1, planes_a, blocks - 2)
    phase(None, None, planes_b, blocks - 1)


def radiate(first, positions, points, coefs, owners):
    freqs, _, depth = coefs.shape
    panels = depth // 4
    observers = points.shape[1]
    lanes = observers // owners
    width = 256
    blocks = observers // width
    return pl.pallas_call(
        functools.partial(radiate_kernel, freqs, panels, width, blocks),
        out_shape=jax.ShapeDtypeStruct((owners, 2 * freqs, lanes), jnp.float32),
        in_specs=[pl.BlockSpec(memory_space=VMEM)] * 4,
        out_specs=pl.BlockSpec(memory_space=VMEM),
        scratch_shapes=[
            pltpu.VMEM((freqs, depth, width), jnp.bfloat16),
            pltpu.VMEM((freqs, depth, width), jnp.bfloat16),
            pltpu.VMEM((width // lanes, freqs * 8, lanes), jnp.float32),
        ],
        compiler_params=pltpu.CompilerParams(vmem_limit_bytes=60 * 1024 * 1024),
        name="radiate",
    )(first, positions, points, coefs)


def enter(axis, count):
    barrier = pltpu.get_barrier_semaphore()
    me = lax.axis_index(axis)
    for step in range(1, count):
        pl.semaphore_signal(
            barrier, inc=1, device_id={axis: lax.rem(me + step, count)}, device_id_type=MESH
        )
    return barrier


def scatter_sum_kernel(owners, part_ref, out_ref, landed, send_sem, recv_sem):
    me = lax.axis_index("panel")
    pl.semaphore_wait(enter("panel", owners), owners - 1)
    copies = []
    for step in range(1, owners):
        peer = lax.rem(me + step, owners)
        copies.append(
            pltpu.make_async_remote_copy(
                src_ref=part_ref.at[peer],
                dst_ref=landed.at[step],
                send_sem=send_sem.at[step],
                recv_sem=recv_sem.at[step],
                device_id={"panel": peer},
                device_id_type=MESH,
            )
        )
        copies[-1].start()
    total = part_ref[me]
    for step in range(1, owners):
        copies[step - 1].wait_recv()
        total = total + landed[step]
    out_ref[...] = total
    for copy in copies:
        copy.wait_send()


def scatter_sum(parts):
    owners, rows, lanes = parts.shape
    return pl.pallas_call(
        functools.partial(scatter_sum_kernel, owners),
        out_shape=jax.ShapeDtypeStruct((rows, lanes), jnp.float32),
        in_specs=[pl.BlockSpec(memory_space=VMEM)],
        out_specs=pl.BlockSpec(memory_space=VMEM),
        scratch_shapes=[
            pltpu.VMEM((owners, rows, lanes), jnp.float32),
            pltpu.SemaphoreType.DMA((owners,)),
            pltpu.SemaphoreType.DMA((owners,)),
        ],
        compiler_params=pltpu.CompilerParams(collective_id=1, has_side_effects=True),
        name="scatter_sum",
    )(parts)


def ground_kernel(chunk, rays, owners, spectrum_ref, absorption_ref, count_ref, layer_ref,
                  length_ref, weight_ref, ground_ref, out_ref, left, total):
    freqs = absorption_ref.shape[0]
    layers = absorption_ref.shape[1]
    observers = spectrum_ref.shape[1]
    low_size = out_ref.shape[2]
    real, imaginary = spectrum_ref[0:freqs, :], spectrum_ref[freqs : 2 * freqs, :]
    power = real * real + imaginary * imaginary
    highest = lax.Precision.HIGHEST

    def step(index, carry):
        at = pl.ds(pl.multiple_of(index * chunk, chunk), chunk)
        layer_ids = lax.broadcasted_iota(jnp.int32, (layers, chunk), 0)
        count = count_ref[0:1, at]
        lengths = jnp.zeros((layers, chunk), jnp.float32)
        for segment in range(layer_ref.shape[0]):
            used = jnp.where(segment < count, length_ref[segment : segment + 1, at], 0.0)
            same = layer_ref[segment : segment + 1, at] == layer_ids
            lengths = lengths + jnp.where(same, used, 0.0)
        depth = jnp.dot(
            absorption_ref[...], lengths, precision=highest, preferred_element_type=jnp.float32
        )
        shape = (observers, chunk)
        start = lax.broadcasted_iota(jnp.int32, shape, 0) * rays - index * chunk
        column = lax.broadcasted_iota(jnp.int32, shape, 1)
        owner = jnp.where((column >= start) & (column < start + rays), 1.0, 0.0)
        spread = jnp.dot(power, owner, precision=highest, preferred_element_type=jnp.float32)
        energy = spread * weight_ref[0:1, at] * jnp.exp(-depth)
        high = energy.astype(jnp.bfloat16)
        low = (energy - high.astype(jnp.float32)).astype(jnp.bfloat16)
        ground = ground_ref[0:1, at]
        block = ground // low_size
        within = ground - block * low_size
        for owner_id in range(owners):
            keep = jnp.where(block == owner_id, 1.0, 0.0).astype(jnp.bfloat16)
            left[2 * owner_id * freqs : (2 * owner_id + 1) * freqs, :] = high * keep
            left[(2 * owner_id + 1) * freqs : (2 * owner_id + 2) * freqs, :] = low * keep
        ids = lax.broadcasted_iota(jnp.int32, (low_size, chunk), 0)
        right = jnp.where(ids == within, 1.0, 0.0).astype(jnp.bfloat16)
        product = lax.dot_general(
            left[...], right, (((1,), (1,)), ((), ())), preferred_element_type=jnp.float32
        )
        total[...] = product + jnp.where(index > 0, total[...], 0.0)
        return carry

    lax.fori_loop(0, count_ref.shape[1] // chunk, step, 0)
    for owner_id in range(owners):
        first = 2 * owner_id * freqs
        out_ref[owner_id] = total[first : first + freqs, :] + total[
            first + freqs : first + 2 * freqs, :
        ]


def ground_parts(spectrum, absorption, count, layer, length, weight, ground, owners):
    freqs = absorption.shape[0]
    rows = count.shape[1]
    chunk = 1024
    low_size = GROUND // owners
    rays = rows // spectrum.shape[1]
    return pl.pallas_call(
        functools.partial(ground_kernel, chunk, rays, owners),
        out_shape=jax.ShapeDtypeStruct((owners, freqs, low_size), jnp.float32),
        in_specs=[pl.BlockSpec(memory_space=VMEM)] * 7,
        out_specs=pl.BlockSpec(memory_space=VMEM),
        scratch_shapes=[
            pltpu.VMEM((2 * owners * freqs, chunk), jnp.bfloat16),
            pltpu.VMEM((2 * owners * freqs, low_size), jnp.float32),
        ],
        compiler_params=pltpu.CompilerParams(vmem_limit_bytes=48 * 1024 * 1024),
        name="ground",
    )(spectrum, absorption, count, layer, length, weight, ground)


def ground_sum_kernel(owners, groups, part_ref, out_ref, landed, mine, others, send_sem, recv_sem,
                      send_group, recv_group):
    me = lax.axis_index("panel")
    group = lax.axis_index("freq")
    freqs = part_ref.shape[1]
    barrier = enter("panel", owners)
    enter("freq", groups)
    pl.semaphore_wait(barrier, owners + groups - 2)
    copies = []
    for step in range(1, owners):
        peer = lax.rem(me + step, owners)
        copies.append(
            pltpu.make_async_remote_copy(
                src_ref=part_ref.at[peer],
                dst_ref=landed.at[step],
                send_sem=send_sem.at[step],
                recv_sem=recv_sem.at[step],
                device_id={"panel": peer},
                device_id_type=MESH,
            )
        )
        copies[-1].start()
    total = part_ref[me]
    for step in range(1, owners):
        copies[step - 1].wait_recv()
        total = total + landed[step]
    mine[...] = total
    across = []
    for step in range(1, groups):
        peer = lax.rem(group + step, groups)
        across.append(
            pltpu.make_async_remote_copy(
                src_ref=mine,
                dst_ref=others.at[step],
                send_sem=send_group.at[step],
                recv_sem=recv_group.at[step],
                device_id={"freq": peer},
                device_id_type=MESH,
            )
        )
        across[-1].start()
    out_ref[pl.ds(pl.multiple_of(group * freqs, freqs), freqs), :] = total
    for copy in copies:
        copy.wait_send()
    for step in range(1, groups):
        across[step - 1].wait_recv()
        source = lax.rem(group + groups - step, groups)
        out_ref[pl.ds(pl.multiple_of(source * freqs, freqs), freqs), :] = others[step]
    for copy in across:
        copy.wait_send()


def ground_sum(parts, groups):
    owners, freqs, lanes = parts.shape
    return pl.pallas_call(
        functools.partial(ground_sum_kernel, owners, groups),
        out_shape=jax.ShapeDtypeStruct((groups * freqs, lanes), jnp.float32),
        in_specs=[pl.BlockSpec(memory_space=VMEM)],
        out_specs=pl.BlockSpec(memory_space=VMEM),
        scratch_shapes=[
            pltpu.VMEM((owners, freqs, lanes), jnp.float32),
            pltpu.VMEM((freqs, lanes), jnp.float32),
            pltpu.VMEM((groups, freqs, lanes), jnp.float32),
            pltpu.SemaphoreType.DMA((owners,)),
            pltpu.SemaphoreType.DMA((owners,)),
            pltpu.SemaphoreType.DMA((groups,)),
            pltpu.SemaphoreType.DMA((groups,)),
        ],
        compiler_params=pltpu.CompilerParams(collective_id=2, has_side_effects=True),
        name="ground_sum",
    )(parts)


def coefficients(spectra, positions, normals, wavenumbers, weighting):
    mono_real, mono_imag, load_real, load_imag = spectra
    wave = (weighting * wavenumbers)[:, None, None]
    distance = jnp.concatenate(
        [1.0 + jnp.sum(positions * positions, axis=0, keepdims=True), -2.0 * positions]
    )[None]
    facing = jnp.concatenate(
        [-jnp.sum(normals * positions, axis=0, keepdims=True), normals]
    )[None]
    near = weighting / RADIUS
    cube_real = -wave * mono_imag[:, None] * distance + near * load_real[:, None] * facing
    cube_imag = wave * mono_real[:, None] * distance + near * load_imag[:, None] * facing
    square_real = -wave * load_imag[:, None] * facing
    square_imag = wave * load_real[:, None] * facing
    real_rows = jnp.concatenate([cube_real, cube_imag, square_real, square_imag], axis=2)
    imag_rows = jnp.concatenate([cube_imag, -cube_real, square_imag, -square_real], axis=2)
    rows = jnp.concatenate([real_rows, imag_rows], axis=1)
    high = lax.reduce_precision(rows, 8, 7)
    return jnp.concatenate([high, rows - high], axis=1).astype(jnp.bfloat16)


def shards(
    sources,
    panel_pos,
    normal_angles,
    observer_angles,
    absorption,
    ray_count,
    ray_layer,
    ray_length,
    ray_weight,
    ray_ground,
):
    groups = lax.axis_size("freq")
    owners = lax.axis_size("panel")
    freqs = absorption.shape[0] // groups
    freq_start = lax.axis_index("freq") * freqs
    table = jnp.asarray(dft_rows(SAMPLES, BIN0, groups, freqs)).astype(jnp.bfloat16)
    partial_value = lax.dot_general(
        table,
        sources.reshape(-1, SAMPLES),
        (((1,), (1,)), ((), ())),
        preferred_element_type=jnp.float32,
    )
    partial_value = partial_value.reshape(2 * groups * freqs, 2, sources.shape[1])
    spectra = lax.all_to_all(partial_value, "freq", split_axis=0, concat_axis=2, tiled=True)
    spectra = (
        spectra[:freqs, 0],
        spectra[freqs:, 0],
        spectra[:freqs, 1],
        spectra[freqs:, 1],
    )
    first = (BIN0 + freq_start).astype(jnp.float32)
    wavenumbers = (first + jnp.arange(freqs, dtype=jnp.float32)) * (2.0 * math.pi / SAMPLES)
    directions = sphere_points(observer_angles, True)
    normals = sphere_points(normal_angles, False)
    positions = panel_pos / RADIUS
    weighting = GAIN / math.sqrt(panel_pos.shape[1] * owners)
    coefs = coefficients(spectra, positions, normals, wavenumbers, weighting)
    ones = jnp.ones((1, directions.shape[1]), jnp.float32)
    points = jnp.concatenate(
        [directions, jnp.zeros((5, directions.shape[1]), jnp.float32)]
        + [ones, directions, ones, directions]
    )
    padded = jnp.pad(positions.T, ((0, 0), (0, 5)))
    parts = radiate(jnp.full((8, 128), first), padded, points, coefs, owners)
    spectrum = scatter_sum(parts)
    obs_spectrum = (
        spectrum.reshape(2, freqs, -1).transpose(2, 1, 0).reshape(-1, 2 * freqs)
    )
    own_absorption = lax.dynamic_slice_in_dim(absorption, freq_start, freqs, 0)
    ground_part = ground_parts(
        spectrum,
        own_absorption,
        ray_count.reshape(1, -1),
        ray_layer,
        ray_length,
        ray_weight.reshape(1, -1),
        ray_ground.reshape(1, -1),
        owners,
    )
    ground_power = ground_sum(ground_part, groups)
    return (obs_spectrum, ground_power)


def solution(mesh):
    return jax.shard_map(
        shards,
        mesh=mesh,
        in_specs=(
            P(None, ("panel", "freq"), None),
            P(None, "panel"),
            P(None, "panel"),
            P(),
            P(),
            P("panel"),
            P(None, "panel"),
            P(None, "panel"),
            P("panel"),
            P("panel"),
        ),
        out_specs=(P("panel", "freq"), P(None, "panel")),
        check_vma=False,
    )
```

time: 655 us -> 133 us (0.20)
  other arithmetic: 453 us -> 2.33 us
  waiting for transfers between devices: 117 us -> 1.25 us
  Pallas kernels: 0 us -> 112 us
  local copies, waits for them, and re-layouts: 32.8 us -> 8.72 us
  loops' own time: 22 us -> 0 us
  between operations: 14.3 us -> 0.9 us
    reduce_sum x34 -> x2, other arithmetic: 379 us -> 0.14 us  [the longest x1 0.12 us: coefficients(): jnp.sum(normals * positions, axis=0, keepdims=True)]
    reduce_scatter x2 -> x0, waiting for transfers between devices: 117 us -> none  [the longest x1 61 us: shards(): lax.psum_scatter(ground_part, 'panel', scatter_dimension=1, tiled=True)]
    pallas_call x0 -> x4, Pallas kernels: none -> 112 us  [the longest x1 65.7 us: radiate(): pl.pallas_call(functools.partial(radiate_kernel, freqs, panels, width, bl...]
    scatter-add x1 -> x0, other arithmetic: 45.7 us -> none  [ground_energy(): return empty.at[:, ray_ground].add(energy.reshape(freq_count, -1))]
    mul x37 -> x3, other arithmetic: 25.4 us -> 0.16 us  [the longest x1 0.08 us: coefficients(): wave * mono_real[:, None] * distance + near * load_imag[:, None] * facing]
    another operation x1 -> x0, loops' own time: 22 us -> none  [radiate(): result = lax.map(one_freq, (wavenumbers, per_freq))]
    dynamic_slice x32 -> x1, local copies, waits for them, and re-layouts: 18.8 us -> 0.08 us  [shards(): own_absorption = lax.dynamic_slice_in_dim(absorption, freq_start, freqs, 0)]
    reshape x5 -> x0, local copies, waits for them, and re-layouts: 7.25 us -> none  [the longest x2 5.22 us: ground_energy(): return empty.at[:, ray_ground].add(energy.reshape(freq_count, -1))]
  transfers between devices with their start and end apart: 3 -> 1, of which waited for: 2 -> 1; matrix products, arithmetic and copies ran while one was open for 1% -> 2% of each run, Pallas kernels for 0% -> 0%
where the time goes in v1:
time: 133 us; the launch traced here: 131 us
  Pallas kernels  112 us (84%)
  local copies, waits for them, and re-layouts  8.72 us (7%)
  starting transfers between devices  4.26 us (3%)
  other arithmetic  2.33 us (2%)
    pallas_call x1, Pallas kernels, radiate(): pl.pallas_call(functools.partial(radiate_kernel, freqs, panels, width, bl...  65.7 us
    pallas_call x1, Pallas kernels, ground_sum(): pl.pallas_call(functools.partial(ground_sum_kernel, owners, groups), out_...  20 us
    pallas_call x1, Pallas kernels, scatter_sum(): pl.pallas_call(functools.partial(scatter_sum_kernel, owners), out_shape=j...  15.9 us
    pallas_call x1, Pallas kernels, ground_parts(): pl.pallas_call(functools.partial(ground_kernel, chunk, rays, owners), out...  10.4 us
    all_to_all x1, starting transfers between devices, shards(): lax.all_to_all(partial_value, 'freq', split_axis=0, concat_axis=2, tiled=...  4.26 us
    unnamed x28, local copies, waits for them, and re-layouts  4.12 us
  transfers between devices with their start and end apart: 1, of which 1 were waited for; matrix products, arithmetic and copies ran while one was open for 2% of the time, Pallas kernels for 0%

profile of v1, /device:TPU:0, one launch (start us, length us, event | category | flops | bytes accessed | tf_op | source)
XLA Modules:
  0.0 130.8 jit_solution(13566938106258350716)
XLA Ops:
  0.6 0.0 copy-start
  0.6 0.0 copy-start.12
  0.7 0.0 copy-start.11
  0.7 0.0 copy-start.9
  0.7 0.0 copy-start.10
  0.7 1.0 copy-done
  1.7 1.3 fusion.6
  2.9 0.8 copy.44
  3.7 4.3 %all-to-all-start = ((f32[128,2,128]{2,1,0:T(2,128)}), f32[128,2,128]{2,1,0:T(2,128)S(1)}, u32[]{:S(2)}, u32[]{:S(2)}) async-start(f32[128,2,128]{2,1,0:T(2,128)} %copy.44), calls=%async_computation | async-start | bytes 262144 | tf_op jit(solution)/shard_map/all_to_all | solution.py:414
  8.0 0.0 copy-done.12
  8.0 0.1 cosine_multiply_fusion.1
  8.1 0.1 copy.47
  8.2 0.0 copy-done.11
  8.2 0.1 copy.43
  8.4 0.1 multiply_reduce_fusion
  8.5 0.0 copy-done.9
  8.5 0.5 cosine_negate_fusion
  9.0 0.0 copy-done.10
  9.0 0.1 constant_dynamic-slice_fusion
  9.1 0.1 copy.52.absorption_ref
  9.2 0.7 pad.4.pos_ref
  9.9 1.4 %concatenate.24.points_ref = f32[16,2048]{1,0:T(8,128)} concatenate(f32[1,2048]{1,0:T(1,128)S(1)} %get-tuple-element.18, f32[1,2048]{1,0:T(1,128)S(1)} %get-tuple-element.17, f32[1,2048]{1,0:T(1,128)S(1)} %get-tuple-element.16, f32[5,2048]{1,0:T(8,128)S(1)} %broadcast_in_dim.7, f32[1,2048]{1,0:T(1,128)S(1)} %broadcast_in_dim.16, f32[1,2048]{1,0:T(1,128)S(1)} %get-tuple-element.18, ...), dimensions={0} | concatenate | bytes 262144 | tf_op jit(solution)/shard_map/concatenate | solution.py:429
  11.3 1.3 all-to-all-done
  12.5 0.1 copy.45
  12.6 0.1 all_to_all.16
  12.7 0.1 fusion.1
  12.8 0.2 multiply_add_fusion.1
  13.0 0.3 reduce-precision_convert_fusion
  13.3 1.1 pad_maximum_fusion.coef_ref
  14.4 0.6 broadcast_in_dim.6.first_ref
  14.9 0.0 copy-start.4
  15.0 0.0 copy-start.8
  15.0 65.7 %radiate.1.part_ref = f32[16,64,128]{2,1,0:T(8,128)} custom-call(f32[8,128]{1,0:T(8,128)} %broadcast_in_dim.6.first_ref, f32[256,8]{1,0:T(8,128)} %pad.4.pos_ref, f32[16,2048]{1,0:T(8,128)} %concatenate.24.points_ref, bf16[32,16,1024]{2,1,0:T(8,128)(2,1)} %pad_maximum_fusion.coef_ref), custom_call_target="tpu_custom_call" | custom-call | tf_op jit(solution)/shard_map/radiate/pallas_call | solution.py:155
  80.7 15.9 %scatter_sum.1.spectrum_ref = f32[64,128]{1,0:T(8,128)} custom-call(f32[16,64,128]{2,1,0:T(8,128)} %radiate.1.part_ref), custom_call_target="tpu_custom_call" | custom-call | tf_op jit(solution)/shard_map/scatter_sum/pallas_call | solution.py:208
  96.6 0.0 copy-done.4
  96.6 0.0 copy-done.5
  96.6 0.0 copy-done.6
  96.6 0.0 copy-done.7
  96.7 0.0 copy-done.8
  96.7 0.0 copy-start.2
  96.7 0.7 copy-done.2
  97.4 10.4 %ground.1.part_ref = f32[16,32,256]{2,1,0:T(8,128)S(1)} custom-call(f32[64,128]{1,0:T(8,128)S(1)} %copy-done.2, f32[32,16]{1,0:T(8,128)S(1)} %copy.52.absorption_ref, s32[1,8192]{1,0:T(1,128)S(1)} %bitcast.31, s32[8,8192]{1,0:T(8,128)S(1)} %copy-done.4, f32[8,8192]{1,0:T(8,128)S(1)} %copy-done.5, f32[1,8192]{1,0:T(1,128)S(1)} %bitcast.32, s32[1,8192]{1,0:T(1,128)S(1)} %bitcast.33), custom_call_target="tpu_custom_call" | custom-call | tf_op jit(solution)/shard_map/ground/pallas_call | solution.py:282
  107.8 0.0 copy-start.1
  107.9 0.8 copy-done.1
  108.6 20.0 %ground_sum.1 = f32[64,256]{1,0:T(8,128)} custom-call(f32[16,32,256]{2,1,0:T(8,128)} %copy-done.1), custom_call_target="tpu_custom_call" | custom-call | tf_op jit(solution)/shard_map/ground_sum/pallas_call | solution.py:350
  128.7 0.0 copy-done.3
  128.7 0.6 copy.49
  129.3 1.5 %copy.54 = f32[64,256]{1,0:T(8,128)} copy(f32[64,256]{1,0:T(8,128)} %ground_sum.1) | data formatting | bytes 131072
  (12 shorter events, 0.1 us)
Async XLA Ops:
  0.6 1.0 copy-start
  0.6 7.3 %copy-start.12 = (f32[2,256]{1,0:T(2,128)S(1)}, f32[2,256]{1,0:T(2,128)}, u32[]{:S(2)}) copy-start(f32[2,256]{1,0:T(2,128)} %param.13) | copy-start | bytes 6148
  0.7 7.5 %copy-start.11 = (f32[3,256]{1,0:T(4,128)S(1)}, f32[3,256]{1,0:T(4,128)}, u32[]{:S(2)}) copy-start(f32[3,256]{1,0:T(4,128)} %param.12) | copy-start | bytes 9220
  0.7 7.9 %copy-start.9 = (f32[2,2048]{1,0:T(2,128)S(1)}, f32[2,2048]{1,0:T(2,128)}, u32[]{:S(2)}) copy-start(f32[2,2048]{1,0:T(2,128)} %param.14) | copy-start | bytes 49156
  0.7 8.3 %copy-start.10 = (f32[64,16]{0,1:T(8,128)S(1)}, f32[64,16]{0,1:T(8,128)}, u32[]{:S(2)}) copy-start(f32[64,16]{0,1:T(8,128)} %param.15) | copy-start | bytes 12292
  3.7 8.8 %all-to-all-start = ((f32[128,2,128]{2,1,0:T(2,128)}), f32[128,2,128]{2,1,0:T(2,128)S(1)}, u32[]{:S(2)}, u32[]{:S(2)}) async-start(f32[128,2,128]{2,1,0:T(2,128)} %copy.44), calls=%async_computation | async-start | bytes 262144 | tf_op jit(solution)/shard_map/all_to_all | solution.py:414
  14.9 81.7 %copy-start.4 = (s32[8,8192]{1,0:T(8,128)S(1)}, s32[8,8192]{1,0:T(8,128)}, u32[]{:S(2)}) copy-start(s32[8,8192]{1,0:T(8,128)} %layer_ref.1) | copy-start | bytes 786436
  15.0 81.7 %copy-start.5 = (f32[8,8192]{1,0:T(8,128)S(1)}, f32[8,8192]{1,0:T(8,128)}, u32[]{:S(2)}) copy-start(f32[8,8192]{1,0:T(8,128)} %length_ref.1) | copy-start | bytes 786436
  15.0 81.7 %copy-start.6 = (s32[8192]{0:T(1024)S(1)}, s32[8192]{0:T(1024)}, u32[]{:S(2)}) copy-start(s32[8192]{0:T(1024)} %param.16) | copy-start | bytes 98308
  15.0 81.7 %copy-start.7 = (f32[8192]{0:T(1024)S(1)}, f32[8192]{0:T(1024)}, u32[]{:S(2)}) copy-start(f32[8192]{0:T(1024)} %param.19) | copy-start | bytes 98308
  15.0 81.7 %copy-start.8 = (s32[8192]{0:T(1024)S(1)}, s32[8192]{0:T(1024)}, u32[]{:S(2)}) copy-start(s32[8192]{0:T(1024)} %param.20) | copy-start | bytes 98308
  96.7 0.8 copy-start.2
  97.4 31.3 %copy-start.3 = (f32[64,128]{1,0:T(8,128)S(1)}, f32[64,128]{1,0:T(8,128)}, u32[]{:S(2)}) copy-start(f32[64,128]{1,0:T(8,128)} %scatter_sum.1.spectrum_ref) | copy-start | bytes 98308
  107.8 0.8 copy-start.1

commit v2 on v1

v2 whole, which is shorter than its diff:
```python
import functools
import math

import jax
import jax.numpy as jnp
import numpy as np
from jax import lax
from jax.experimental import pallas as pl
from jax.experimental.pallas import tpu as pltpu
from jax.sharding import PartitionSpec as P

SAMPLES = 1024
BIN0 = 32
RADIUS = 150.0
GAIN = 3.0
GROUND = 4096
TILE = 16
MESH = pl.DeviceIdType.MESH
VMEM = pltpu.MemorySpace.VMEM


def dft_rows(samples, first_bin, groups, per_group):
    index = np.arange(samples)
    bins = first_bin + np.arange(groups * per_group)
    angle = 2.0 * np.pi / samples * (bins[:, None] * index[None, :] % samples)
    window = (0.5 - 0.5 * np.cos(2.0 * np.pi / samples * index)) / math.sqrt(samples)
    rows = np.stack([window * np.cos(angle), -window * np.sin(angle)])
    rows = rows.reshape(2, groups, per_group, samples).transpose(1, 0, 2, 3)
    return rows.reshape(-1, samples).astype(np.float32)


def sphere_points(angles, downward):
    polar, azimuth = angles[0], angles[1]
    height = -jnp.cos(polar) if downward else jnp.cos(polar)
    return jnp.stack(
        [jnp.sin(polar) * jnp.cos(azimuth), jnp.sin(polar) * jnp.sin(azimuth), height]
    )


def sincos_turns(turns):
    part = turns - jnp.round(turns)
    square = part * part
    sine = jnp.float32(-(math.pi**11) / math.factorial(11))
    for power in (9, 7, 5, 3, 1):
        sign = 1.0 if power % 4 == 1 else -1.0
        sine = sine * square + sign * math.pi**power / math.factorial(power)
    sine = sine * part
    cosine = jnp.float32(math.pi**12 / math.factorial(12))
    for power in (10, 8, 6, 4, 2, 0):
        sign = 1.0 if power % 4 == 0 else -1.0
        cosine = cosine * square + sign * math.pi**power / math.factorial(power)
    return 1.0 - 2.0 * sine * sine, 2.0 * sine * cosine


def enter(axis, count):
    barrier = pltpu.get_barrier_semaphore()
    me = lax.axis_index(axis)
    for step in range(1, count):
        pl.semaphore_signal(
            barrier, inc=1, device_id={axis: lax.rem(me + step, count)}, device_id_type=MESH
        )
    return barrier


def radiate_kernel(freqs, panels, width, blocks, pos_ref, points_ref, coef_ref, out_ref,
                   planes_a, planes_b, stage, parts, landed, send_sem, recv_sem):
    tiles = panels // TILE
    owners, _, lanes = parts.shape
    half = width // lanes
    me = lax.axis_index("panel")
    first = (BIN0 + lax.axis_index("freq") * freqs).astype(jnp.float32)
    start = lax.div(me, half) + 1
    barrier = enter("panel", owners)

    def block_of(order):
        return lax.rem(start + order, blocks)

    def transfer(source, target):
        return pltpu.make_async_remote_copy(
            src_ref=parts.at[target],
            dst_ref=landed.at[source],
            send_sem=send_sem.at[target],
            recv_sem=recv_sem.at[source],
            device_id={"panel": target},
            device_id_type=MESH,
        )

    def generate(planes, order, tile):
        rows = pl.ds(pl.multiple_of(tile * TILE, TILE), TILE)
        cols = pl.ds(pl.multiple_of(block_of(order) * width, width), width)
        total = None
        for axis in range(3):
            diff = points_ref[axis : axis + 1, cols] - pos_ref[rows, axis : axis + 1]
            total = diff * diff if total is None else total + diff * diff
        inverse = lax.rsqrt(total)
        inverse = inverse * (1.5 - 0.5 * total * inverse * inverse)
        turn = total * inverse * jnp.float32(RADIUS / SAMPLES)
        cos_step, sin_step = sincos_turns(turn)
        cos_now, sin_now = sincos_turns(turn * first)
        square = inverse * inverse
        cos_now, sin_now = cos_now * square, sin_now * square
        cos_next = cos_now * cos_step - sin_now * sin_step
        sin_next = sin_now * cos_step + cos_now * sin_step
        twice = 2.0 * cos_step
        for f in range(freqs):
            values = [cos_now * inverse, sin_now * inverse, cos_now, sin_now]
            for part in range(4):
                at = pl.ds(pl.multiple_of(part * panels + tile * TILE, TILE), TILE)
                planes[f, at, :] = values[part].astype(jnp.bfloat16)
            if f + 1 < freqs:
                cos_now, cos_next = cos_next, twice * cos_next - cos_now
                sin_now, sin_next = sin_next, twice * sin_next - sin_now

    def contract(planes, order, f):
        cols = pl.ds(pl.multiple_of(block_of(order) * width, width), width)
        product = jnp.dot(coef_ref[f], planes[f], preferred_element_type=jnp.float32)
        product = (product[0:8] + product[8:16]) * points_ref[8:16, cols]
        product = product + pltpu.roll(product, 1, axis=0)
        product = product + pltpu.roll(product, 2, axis=0)
        for side in range(half):
            stage[side, pl.ds(pl.multiple_of(f * 8, 8), 8), :] = product[
                :, side * lanes : (side + 1) * lanes
            ]

    def finish(order):
        for side in range(half):
            target = block_of(order) * half + side
            for part in range(2):
                parts[target, part * freqs : (part + 1) * freqs, :] = stage[
                    side, pl.ds(4 * part + 3, freqs, 8), :
                ]

            @pl.when(target != me)
            def _():
                transfer(me, target).start()

    def phase(generated, generated_order, used, used_order):
        if generated is not None and used is not None and freqs % tiles == 0:
            each = freqs // tiles

            def both(tile, carry):
                for n in range(each):
                    contract(used, used_order, tile * each + n)
                generate(generated, generated_order, tile)
                return carry

            lax.fori_loop(0, tiles, both, 0)
            finish(used_order)
            return
        if generated is not None:

            def only_generate(tile, carry):
                generate(generated, generated_order, tile)
                return carry

            lax.fori_loop(0, tiles, only_generate, 0)
        if used is not None:

            def only_contract(f, carry):
                contract(used, used_order, f)
                return carry

            lax.fori_loop(0, freqs, only_contract, 0)
            finish(used_order)

    phase(planes_a, 0, None, None)
    pl.semaphore_wait(barrier, owners - 1)

    def pair(step, carry):
        phase(planes_b, 2 * step + 1, planes_a, 2 * step)
        phase(planes_a, 2 * step + 2, planes_b, 2 * step + 1)
        return carry

    lax.fori_loop(0, blocks // 2 - 1, pair, 0)
    phase(planes_b, blocks - 1, planes_a, blocks - 2)
    phase(None, None, planes_b, blocks - 1)
    total = parts[me]
    for step in range(1, owners):
        source = lax.rem(me + step, owners)
        transfer(source, source).wait_recv()
        total = total + landed[source]
    out_ref[...] = total
    for step in range(1, owners):
        target = lax.rem(me + step, owners)
        transfer(target, target).wait_send()


def radiate(positions, points, coefs, owners):
    freqs, _, depth = coefs.shape
    panels = depth // 4
    observers = points.shape[1]
    lanes = observers // owners
    width = 256
    blocks = observers // width
    return pl.pallas_call(
        functools.partial(radiate_kernel, freqs, panels, width, blocks),
        out_shape=jax.ShapeDtypeStruct((2 * freqs, lanes), jnp.float32),
        in_specs=[pl.BlockSpec(memory_space=VMEM)] * 3,
        out_specs=pl.BlockSpec(memory_space=VMEM),
        scratch_shapes=[
            pltpu.VMEM((freqs, depth, width), jnp.bfloat16),
            pltpu.VMEM((freqs, depth, width), jnp.bfloat16),
            pltpu.VMEM((width // lanes, freqs * 8, lanes), jnp.float32),
            pltpu.VMEM((owners, 2 * freqs, lanes), jnp.float32),
            pltpu.VMEM((owners, 2 * freqs, lanes), jnp.float32),
            pltpu.SemaphoreType.DMA((owners,)),
            pltpu.SemaphoreType.DMA((owners,)),
        ],
        compiler_params=pltpu.CompilerParams(
            vmem_limit_bytes=60 * 1024 * 1024, collective_id=1, has_side_effects=True
        ),
        name="radiate",
    )(positions, points, coefs)


def ground_kernel(chunk, rays, owners, groups, each, spectrum_ref, absorption_ref, count_ref,
                  layer_ref, length_ref, weight_ref, ground_ref, out_ref, energies, lows, left,
                  total, own, parts, landed, mine, others, send_sem, recv_sem, send_group,
                  recv_group):
    freqs = absorption_ref.shape[0]
    layers = absorption_ref.shape[1]
    observers = spectrum_ref.shape[1]
    low_size = out_ref.shape[1]
    me = lax.axis_index("panel")
    group = lax.axis_index("freq")
    barrier = enter("panel", owners)
    enter("freq", groups)
    real, imaginary = spectrum_ref[0:freqs, :], spectrum_ref[freqs : 2 * freqs, :]
    power = real * real + imaginary * imaginary
    highest = lax.Precision.HIGHEST
    chunks = count_ref.shape[1] // chunk

    def transfer(source, target):
        return pltpu.make_async_remote_copy(
            src_ref=parts.at[target],
            dst_ref=landed.at[source],
            send_sem=send_sem.at[target],
            recv_sem=recv_sem.at[source],
            device_id={"panel": target},
            device_id_type=MESH,
        )

    def prepare(index, carry):
        at = pl.ds(pl.multiple_of(index * chunk, chunk), chunk)
        layer_ids = lax.broadcasted_iota(jnp.int32, (layers, chunk), 0)
        count = count_ref[0:1, at]
        lengths = jnp.zeros((layers, chunk), jnp.float32)
        for segment in range(layer_ref.shape[0]):
            used = jnp.where(segment < count, length_ref[segment : segment + 1, at], 0.0)
            same = layer_ref[segment : segment + 1, at] == layer_ids
            lengths = lengths + jnp.where(same, used, 0.0)
        depth = jnp.dot(
            absorption_ref[...], lengths, precision=highest, preferred_element_type=jnp.float32
        )
        shape = (observers, chunk)
        start = lax.broadcasted_iota(jnp.int32, shape, 0) * rays - index * chunk
        column = lax.broadcasted_iota(jnp.int32, shape, 1)
        owner = jnp.where((column >= start) & (column < start + rays), 1.0, 0.0)
        spread = jnp.dot(power, owner, precision=highest, preferred_element_type=jnp.float32)
        energy = spread * weight_ref[0:1, at] * jnp.exp(-depth)
        high = energy.astype(jnp.bfloat16)
        energies[0:freqs, at] = high
        energies[freqs : 2 * freqs, at] = (energy - high.astype(jnp.float32)).astype(jnp.bfloat16)
        within = ground_ref[0:1, at] & (low_size - 1)
        ids = lax.broadcasted_iota(jnp.int32, (low_size, chunk), 0)
        lows[:, at] = jnp.where(ids == within, 1.0, 0.0).astype(jnp.bfloat16)
        return carry

    lax.fori_loop(0, chunks, prepare, 0)
    pl.semaphore_wait(barrier, owners + groups - 2)

    def batch(order, carry):
        base = lax.rem(lax.div(me, each) + 1 + order, owners // each) * each
        total[...] = jnp.zeros_like(total)

        def step(index, carry):
            at = pl.ds(pl.multiple_of(index * chunk, chunk), chunk)
            block = ground_ref[0:1, at] // low_size
            for n in range(each):
                keep = jnp.where(block == base + n, 1.0, 0.0).astype(jnp.bfloat16)
                left[2 * n * freqs : 2 * (n + 1) * freqs, :] = energies[:, at] * keep
            total[...] += lax.dot_general(
                left[...],
                lows[:, at],
                (((1,), (1,)), ((), ())),
                preferred_element_type=jnp.float32,
            )
            return carry

        lax.fori_loop(0, chunks, step, 0)
        for n in range(each):
            target = base + n
            middle = (2 * n + 1) * freqs
            value = total[middle - freqs : middle, :] + total[middle : middle + freqs, :]
            parts[target] = value.astype(jnp.bfloat16)

            @pl.when(target != me)
            def _():
                transfer(me, target).start()

            @pl.when(target == me)
            def _():
                own[...] = value

        return carry

    lax.fori_loop(0, owners // each, batch, 0)
    value = own[...]
    for step in range(1, owners):
        source = lax.rem(me + step, owners)
        transfer(source, source).wait_recv()
        value = value + landed[source].astype(jnp.float32)
    mine[...] = value
    across = []
    for step in range(1, groups):
        peer = lax.rem(group + step, groups)
        across.append(
            pltpu.make_async_remote_copy(
                src_ref=mine,
                dst_ref=others.at[step],
                send_sem=send_group.at[step],
                recv_sem=recv_group.at[step],
                device_id={"freq": peer},
                device_id_type=MESH,
            )
        )
        across[-1].start()
    out_ref[pl.ds(pl.multiple_of(group * freqs, freqs), freqs), :] = value
    for step in range(1, owners):
        target = lax.rem(me + step, owners)
        transfer(target, target).wait_send()
    for step in range(1, groups):
        across[step - 1].wait_recv()
        source = lax.rem(group + groups - step, groups)
        out_ref[pl.ds(pl.multiple_of(source * freqs, freqs), freqs), :] = others[step]
    for copy in across:
        copy.wait_send()


def ground_sums(spectrum, absorption, count, layer, length, weight, ground, owners, groups):
    freqs = absorption.shape[0]
    rows = count.shape[1]
    chunk = 1024
    low_size = GROUND // owners
    rays = rows // spectrum.shape[1]
    each = min(4, owners)
    return pl.pallas_call(
        functools.partial(ground_kernel, chunk, rays, owners, groups, each),
        out_shape=jax.ShapeDtypeStruct((groups * freqs, low_size), jnp.float32),
        in_specs=[pl.BlockSpec(memory_space=VMEM)] * 7,
        out_specs=pl.BlockSpec(memory_space=VMEM),
        scratch_shapes=[
            pltpu.VMEM((2 * freqs, rows), jnp.bfloat16),
            pltpu.VMEM((low_size, rows), jnp.bfloat16),
            pltpu.VMEM((2 * each * freqs, chunk), jnp.bfloat16),
            pltpu.VMEM((2 * each * freqs, low_size), jnp.float32),
            pltpu.VMEM((freqs, low_size), jnp.float32),
            pltpu.VMEM((owners, freqs, low_size), jnp.bfloat16),
            pltpu.VMEM((owners, freqs, low_size), jnp.bfloat16),
            pltpu.VMEM((freqs, low_size), jnp.float32),
            pltpu.VMEM((groups, freqs, low_size), jnp.float32),
            pltpu.SemaphoreType.DMA((owners,)),
            pltpu.SemaphoreType.DMA((owners,)),
            pltpu.SemaphoreType.DMA((groups,)),
            pltpu.SemaphoreType.DMA((groups,)),
        ],
        compiler_params=pltpu.CompilerParams(
            vmem_limit_bytes=48 * 1024 * 1024, collective_id=2, has_side_effects=True
        ),
        name="ground",
    )(spectrum, absorption, count, layer, length, weight, ground)


def coefficients(spectra, positions, normals, wavenumbers, weighting):
    mono_real, mono_imag, load_real, load_imag = spectra
    wave = (weighting * wavenumbers)[:, None, None]
    distance = jnp.concatenate(
        [1.0 + jnp.sum(positions * positions, axis=0, keepdims=True), -2.0 * positions]
    )[None]
    facing = jnp.concatenate(
        [-jnp.sum(normals * positions, axis=0, keepdims=True), normals]
    )[None]
    near = weighting / RADIUS
    cube_real = -wave * mono_imag[:, None] * distance + near * load_real[:, None] * facing
    cube_imag = wave * mono_real[:, None] * distance + near * load_imag[:, None] * facing
    square_real = -wave * load_imag[:, None] * facing
    square_imag = wave * load_real[:, None] * facing
    real_rows = jnp.concatenate([cube_real, cube_imag, square_real, square_imag], axis=2)
    imag_rows = jnp.concatenate([cube_imag, -cube_real, square_imag, -square_real], axis=2)
    rows = jnp.concatenate([real_rows, imag_rows], axis=1)
    high = lax.reduce_precision(rows, 8, 7)
    return jnp.concatenate([high, rows - high], axis=1).astype(jnp.bfloat16)


def shards(
    sources,
    panel_pos,
    normal_angles,
    observer_angles,
    absorption,
    ray_count,
    ray_layer,
    ray_length,
    ray_weight,
    ray_ground,
):
    groups = lax.axis_size("freq")
    owners = lax.axis_size("panel")
    freqs = absorption.shape[0] // groups
    freq_start = lax.axis_index("freq") * freqs
    table = jnp.asarray(dft_rows(SAMPLES, BIN0, groups, freqs)).astype(jnp.bfloat16)
    partial_value = lax.dot_general(
        table,
        sources.reshape(-1, SAMPLES),
        (((1,), (1,)), ((), ())),
        preferred_element_type=jnp.float32,
    )
    partial_value = partial_value.reshape(2 * groups * freqs, 2, sources.shape[1])
    spectra = lax.all_to_all(partial_value, "freq", split_axis=0, concat_axis=2, tiled=True)
    spectra = (
        spectra[:freqs, 0],
        spectra[freqs:, 0],
        spectra[:freqs, 1],
        spectra[freqs:, 1],
    )
    first = (BIN0 + freq_start).astype(jnp.float32)
    wavenumbers = (first + jnp.arange(freqs, dtype=jnp.float32)) * (2.0 * math.pi / SAMPLES)
    directions = sphere_points(observer_angles, True)
    normals = sphere_points(normal_angles, False)
    positions = panel_pos / RADIUS
    weighting = GAIN / math.sqrt(panel_pos.shape[1] * owners)
    coefs = coefficients(spectra, positions, normals, wavenumbers, weighting)
    ones = jnp.ones((1, directions.shape[1]), jnp.float32)
    points = jnp.concatenate(
        [directions, jnp.zeros((5, directions.shape[1]), jnp.float32)]
        + [ones, directions, ones, directions]
    )
    spectrum = radiate(positions.T, points, coefs, owners)
    obs_spectrum = (
        spectrum.reshape(2, freqs, -1).transpose(2, 1, 0).reshape(-1, 2 * freqs)
    )
    own_absorption = lax.dynamic_slice_in_dim(absorption, freq_start, freqs, 0)
    ground_power = ground_sums(
        spectrum,
        own_absorption,
        ray_count.reshape(1, -1),
        ray_layer,
        ray_length,
        ray_weight.reshape(1, -1),
        ray_ground.reshape(1, -1),
        owners,
        groups,
    )
    return (obs_spectrum, ground_power)


def solution(mesh):
    return jax.shard_map(
        shards,
        mesh=mesh,
        in_specs=(
            P(None, ("panel", "freq"), None),
            P(None, "panel"),
            P(None, "panel"),
            P(),
            P(),
            P("panel"),
            P(None, "panel"),
            P(None, "panel"),
            P("panel"),
            P("panel"),
        ),
        out_specs=(P("panel", "freq"), P(None, "panel")),
        check_vma=False,
    )
```

time: 133 us -> 94.4 us (0.71); the launches traced: 131 us -> 94 us
  Pallas kernels: 112 us -> 77.5 us
  local copies, waits for them, and re-layouts: 8.72 us -> 5.86 us
    pallas_call x3 -> x1, Pallas kernels: 46.4 us -> 23.2 us  [ground_sums(): pl.pallas_call(functools.partial(ground_kernel, chunk, rays, owners, grou...]
    pallas_call x1, Pallas kernels: 65.7 us -> 54.3 us  [radiate(): pl.pallas_call(functools.partial(radiate_kernel, freqs, panels, width, bl...]
    unnamed x28 -> x26, local copies, waits for them, and re-layouts: 4.12 us -> 2.5 us
  transfers between devices with their start and end apart: 1 -> 1, of which waited for: 1 -> 1; matrix products, arithmetic and copies ran while one was open for 2% -> 3% of each run, Pallas kernels for 0% -> 0%
where the time goes in v2:
time: 94.4 us; the launch traced here: 94 us
  Pallas kernels  77.5 us (82%)
  local copies, waits for them, and re-layouts  5.86 us (6%)
  starting transfers between devices  4.26 us (5%)
  other arithmetic  2.32 us (2%)
  waiting for transfers between devices  1.89 us (2%)
  matrix products  1.26 us (1%)
    pallas_call x1, Pallas kernels, radiate(): pl.pallas_call(functools.partial(radiate_kernel, freqs, panels, width, bl...  54.3 us
    pallas_call x1, Pallas kernels, ground_sums(): pl.pallas_call(functools.partial(ground_kernel, chunk, rays, owners, grou...  23.2 us
    all_to_all x1, starting transfers between devices, shards(): lax.all_to_all(partial_value, 'freq', split_axis=0, concat_axis=2, tiled=...  4.26 us
    unnamed x26, local copies, waits for them, and re-layouts  2.5 us
    all_to_all x1, waiting for transfers between devices, shards(): lax.all_to_all(partial_value, 'freq', split_axis=0, concat_axis=2, tiled=...  1.89 us
  transfers between devices with their start and end apart: 1, of which 1 were waited for; matrix products, arithmetic and copies ran while one was open for 3% of the time, Pallas kernels for 0%

profile of v2, /device:TPU:0, one launch (start us, length us, event | category | flops | bytes accessed | tf_op | source)
XLA Modules:
  0.0 94.0 jit_solution(8272606246192305012)
XLA Ops:
  0.6 0.0 copy-start
  0.6 0.0 copy-start.11
  0.7 0.0 copy-start.10
  0.7 0.0 copy-start.8
  0.7 0.0 copy-start.9
  0.7 1.0 %copy-done = bf16[2,128,1024]{2,1,0:T(8,128)(2,1)S(1)} copy-done((bf16[2,128,1024]{2,1,0:T(8,128)(2,1)S(1)}, bf16[2,128,1024]{2,1,0:T(8,128)(2,1)}, u32[]{:S(2)}) %copy-start) | copy-done | bytes 524312
  1.7 1.3 %fusion.6 = f32[128,2,128]{2,0,1:T(8,128)S(1)} fusion(bf16[128,1024,1]{1,0,2:T(8,128)(2,1)} %constant.32, bf16[2,128,1024]{2,1,0:T(8,128)(2,1)S(1)} %copy-done), kind=kOutput, calls=%fused_computation.38 | convolution fusion | flops 67108864 | bytes 917504 | tf_op jit(solution)/shard_map/dot_general | solution.py:412
  2.9 0.8 copy.44
  3.7 4.3 %all-to-all-start = ((f32[128,2,128]{2,1,0:T(2,128)}), f32[128,2,128]{2,1,0:T(2,128)S(1)}, u32[]{:S(2)}, u32[]{:S(2)}) async-start(f32[128,2,128]{2,1,0:T(2,128)} %copy.44), calls=%async_computation | async-start | bytes 262144 | tf_op jit(solution)/shard_map/all_to_all | solution.py:419
  8.0 0.0 copy-done.11
  8.0 0.1 cosine_multiply_fusion.1
  8.1 0.1 copy.47
  8.2 0.0 copy-done.10
  8.2 0.1 copy.43
  8.4 0.0 copy-start.7
  8.4 0.1 multiply_reduce_fusion
  8.5 0.0 copy-done.8
  8.5 0.5 cosine_negate_fusion
  9.0 0.0 copy-done.9
  9.0 0.1 constant_dynamic-slice_fusion
  9.1 0.1 copy.52.absorption_ref
  9.2 1.4 %concatenate.24.points_ref = f32[16,2048]{1,0:T(8,128)} concatenate(f32[1,2048]{1,0:T(1,128)S(1)} %get-tuple-element.18, f32[1,2048]{1,0:T(1,128)S(1)} %get-tuple-element.17, f32[1,2048]{1,0:T(1,128)S(1)} %get-tuple-element.16, f32[5,2048]{1,0:T(8,128)S(1)} %broadcast_in_dim.4, f32[1,2048]{1,0:T(1,128)S(1)} %broadcast_in_dim.5, f32[1,2048]{1,0:T(1,128)S(1)} %get-tuple-element.18, ...), dimensions={0} | concatenate | bytes 262144 | tf_op jit(solution)/shard_map/concatenate | solution.py:434
  10.6 1.9 %all-to-all-done = f32[128,2,128]{2,1,0:T(2,128)S(1)} async-done(((f32[128,2,128]{2,1,0:T(2,128)}), f32[128,2,128]{2,1,0:T(2,128)S(1)}, u32[]{:S(2)}, u32[]{:S(2)}) %all-to-all-start) | async-done | bytes 131104 | tf_op jit(solution)/shard_map/all_to_all | solution.py:419
  12.5 0.1 copy.45
  12.6 0.1 all_to_all.16
  12.7 0.1 fusion.1
  12.8 0.2 multiply_add_fusion.1
  13.0 0.0 copy-done.7
  13.0 0.3 reduce-precision_convert_fusion
  13.3 1.1 %pad_maximum_fusion.coef_ref = bf16[32,16,1024]{2,1,0:T(8,128)(2,1)} fusion(bf16[32,8,1024]{2,1,0:T(8,128)(2,1)S(1)} %get-tuple-element.3, bf16[32,8,1024]{2,1,0:T(8,128)(2,1)S(1)} %get-tuple-element.2), kind=kLoop, calls=%fused_computation.4 | loop fusion | flops 2097152 | bytes 2097152 | tf_op jit(solution)/shard_map/concatenate | solution.py:392
  14.4 0.0 copy-start.2
  14.4 0.0 copy-start.3
  14.4 0.0 copy-start.4
  14.4 0.0 copy-start.5
  14.4 0.0 copy-start.6
  14.4 54.3 %radiate.1.spectrum_ref = f32[64,128]{1,0:T(8,128)} custom-call(f32[256,3]{1,0:T(8,128)} %bitcast.34, f32[16,2048]{1,0:T(8,128)} %concatenate.24.points_ref, bf16[32,16,1024]{2,1,0:T(8,128)(2,1)} %pad_maximum_fusion.coef_ref), custom_call_target="tpu_custom_call" | custom-call | tf_op jit(solution)/shard_map/radiate/pallas_call | solution.py:195
  68.7 0.0 copy-done.2
  68.7 0.0 copy-done.3
  68.7 0.0 copy-done.4
  68.8 0.0 copy-done.5
  68.8 0.0 copy-done.6
  68.8 0.0 copy-start.1
  68.8 0.7 copy-done.1
  69.5 23.2 %ground.1 = f32[64,256]{1,0:T(8,128)S(1)} custom-call(f32[64,128]{1,0:T(8,128)S(1)} %copy-done.1, f32[32,16]{1,0:T(8,128)S(1)} %copy.52.absorption_ref, s32[1,8192]{1,0:T(1,128)S(1)} %bitcast.31, s32[8,8192]{1,0:T(8,128)S(1)} %copy-done.2, f32[8,8192]{1,0:T(8,128)S(1)} %copy-done.3, f32[1,8192]{1,0:T(1,128)S(1)} %bitcast.32, s32[1,8192]{1,0:T(1,128)S(1)} %bitcast.33), custom_call_target="tpu_custom_call" | custom-call | tf_op jit(solution)/shard_map/ground/pallas_call | solution.py:347
  92.8 0.6 copy.49
  93.4 0.6 copy.54
  (8 shorter events, 0.1 us)
Async XLA Ops:
  0.6 1.0 %copy-start = (bf16[2,128,1024]{2,1,0:T(8,128)(2,1)S(1)}, bf16[2,128,1024]{2,1,0:T(8,128)(2,1)}, u32[]{:S(2)}) copy-start(bf16[2,128,1024]{2,1,0:T(8,128)(2,1)} %param.11) | copy-start | bytes 1572868
  0.6 7.3 %copy-start.11 = (f32[2,256]{1,0:T(2,128)S(1)}, f32[2,256]{1,0:T(2,128)}, u32[]{:S(2)}) copy-start(f32[2,256]{1,0:T(2,128)} %param.13) | copy-start | bytes 6148
  0.7 7.6 %copy-start.10 = (f32[3,256]{1,0:T(4,128)S(1)}, f32[3,256]{1,0:T(4,128)}, u32[]{:S(2)}) copy-start(f32[3,256]{1,0:T(4,128)} %param.12) | copy-start | bytes 9220
  0.7 7.9 %copy-start.8 = (f32[2,2048]{1,0:T(2,128)S(1)}, f32[2,2048]{1,0:T(2,128)}, u32[]{:S(2)}) copy-start(f32[2,2048]{1,0:T(2,128)} %param.14) | copy-start | bytes 49156
  0.7 8.3 %copy-start.9 = (f32[64,16]{0,1:T(8,128)S(1)}, f32[64,16]{0,1:T(8,128)}, u32[]{:S(2)}) copy-start(f32[64,16]{0,1:T(8,128)} %param.15) | copy-start | bytes 12292
  3.7 8.8 %all-to-all-start = ((f32[128,2,128]{2,1,0:T(2,128)}), f32[128,2,128]{2,1,0:T(2,128)S(1)}, u32[]{:S(2)}, u32[]{:S(2)}) async-start(f32[128,2,128]{2,1,0:T(2,128)} %copy.44), calls=%async_computation | async-start | bytes 262144 | tf_op jit(solution)/shard_map/all_to_all | solution.py:419
  8.4 4.6 %copy-start.7 = (f32[3,256]{0,1:T(8,128)}, f32[3,256]{0,1:T(8,128)S(1)}, u32[]{:S(2)}) copy-start(f32[3,256]{0,1:T(8,128)S(1)} %copy.43) | copy-start | bytes 9220
  14.4 54.4 %copy-start.2 = (s32[8,8192]{1,0:T(8,128)S(1)}, s32[8,8192]{1,0:T(8,128)}, u32[]{:S(2)}) copy-start(s32[8,8192]{1,0:T(8,128)} %layer_ref.1) | copy-start | bytes 786436
  14.4 54.4 %copy-start.3 = (f32[8,8192]{1,0:T(8,128)S(1)}, f32[8,8192]{1,0:T(8,128)}, u32[]{:S(2)}) copy-start(f32[8,8192]{1,0:T(8,128)} %length_ref.1) | copy-start | bytes 786436
  14.4 54.4 %copy-start.4 = (s32[8192]{0:T(1024)S(1)}, s32[8192]{0:T(1024)}, u32[]{:S(2)}) copy-start(s32[8192]{0:T(1024)} %param.16) | copy-start | bytes 98308
  14.4 54.4 %copy-start.5 = (f32[8192]{0:T(1024)S(1)}, f32[8192]{0:T(1024)}, u32[]{:S(2)}) copy-start(f32[8192]{0:T(1024)} %param.19) | copy-start | bytes 98308
  14.4 54.4 %copy-start.6 = (s32[8192]{0:T(1024)S(1)}, s32[8192]{0:T(1024)}, u32[]{:S(2)}) copy-start(s32[8192]{0:T(1024)} %param.20) | copy-start | bytes 98308
  68.8 0.8 copy-start.1
